TPU v7x, 256 devices: a whole 4x4x8 slice. The times are simulated.
256 devices in a mesh: scen: 16 (over y, x), lx: 4 (over z_lo, core), ly: 4 (over z_hi).
Axes of the slice: x: 4, y: 4, z: 8 (z_hi: 4, z_lo: 2; z = z_hi * 2 + z_lo), core: 2. Of those that a mesh axis runs over, the one named last changes fastest.
Arguments:
- density: float32 [16, 512, 2048], P('scen', 'lx', 'ly'), may hold values from 0.2 to 1.5
- trait: float32 [16, 512, 2048], P('scen', 'lx', 'ly'), may hold values from -4 to 4
- variance: float32 [16, 512, 2048], P('scen', 'lx', 'ly'), may hold values from 0.1 to 1
- optimum: float32 [16, 512, 2048], P('scen', 'lx', 'ly'), may hold values from -4 to 4
- observed: float32 [16, 512, 2048], P('scen', 'lx', 'ly'), may hold values from 0 to 1.5
- obs_step: int32 [16, 512], P('scen', 'lx'), may hold values from 1 to 2
- land_code: int32 [512, 2048], P('lx', 'ly'), may hold values 0 or 1
- maps: float32 [2, 512, 2048], P(None, 'lx', 'ly'), may hold values from -4 to 4
- first_moment: float32 [2, 512, 2048], P(None, 'lx', 'ly'), may hold values from -3 to 3
- second_moment: float32 [2, 512, 2048], P(None, 'lx', 'ly'), may hold values from 0.01 to 1
Outputs:
- new_maps: float32 [2, 512, 2048], P(None, 'lx', 'ly')
- new_first: float32 [2, 512, 2048], P(None, 'lx', 'ly')
- new_second: float32 [2, 512, 2048], P(None, 'lx', 'ly')
Inputs may be any that keep to these rules, and one draw needn't show every extreme that they name: `land_code`: 1 marks land, 0 sea.
All inputs are finite; a program needn't handle non-finite values. No bound on the sum of `land_code` on one device may be relied on, other than what follows from the above.
Results may differ from a plain program's by a relative error of at most 0.0003.
Values sent between devices are 32-bit elements; how exact they have to be, the bound alone decides.
A program may use at most 64 MiB of HBM per device.

v0:
```python
import jax
import jax.numpy as jnp
from jax import lax
from jax.sharding import PartitionSpec as P

STEPS = 2
ADAM_STEP = 10


REACH_MAX = 0.2
PRIOR_WEIGHT = 0.1
GROWTH_RATE = 0.5
MUTATION_INPUT = 0.02
LEARN_RATE = 0.01
BETA_FIRST = 0.9
BETA_SECOND = 0.999
ADAM_EPS = 1e-08
LOSS_WEIGHT = 2.0


def extended(block, sides, width):
    for axis, dim in sides:
        count = lax.axis_size(axis)
        forward = [(i, i + 1) for i in range(count - 1)]
        backward = [(target, source) for source, target in forward]
        low = lax.ppermute(
            lax.slice_in_dim(block, block.shape[dim] - width, None, axis=dim), axis, forward
        )
        high = lax.ppermute(lax.slice_in_dim(block, 0, width, axis=dim), axis, backward)
        block = jnp.concatenate([low, block, high], axis=dim)
    return block


def interior(values):
    return values[..., 1:-1, 1:-1]


def advance(fields, raw_maps, optimum_map, land_frac):
    density_now, trait_now, variance_now = (fields[0], fields[1], fields[2])
    reach_map = REACH_MAX * jax.nn.sigmoid(raw_maps[0])
    selection = jax.nn.softplus(interior(raw_maps[1]))
    carried = density_now * trait_now
    moment_two = density_now * (variance_now + trait_now * trait_now)
    reach_mid = interior(reach_map)
    land_mid = interior(land_frac)
    cuts = (
        (slice(2, None), slice(1, -1)),
        (slice(None, -2), slice(1, -1)),
        (slice(1, -1), slice(2, None)),
        (slice(1, -1), slice(None, -2)),
    )
    spread_density = interior(density_now)
    spread_carried = interior(carried)
    spread_moment = interior(moment_two)
    for row_cut, col_cut in cuts:
        weight = (
            0.5 * (reach_mid + reach_map[row_cut, col_cut]) * land_mid * land_frac[row_cut, col_cut]
        )
        spread_density = spread_density + weight * (
            density_now[row_cut, col_cut] - interior(density_now)
        )
        spread_carried = spread_carried + weight * (carried[row_cut, col_cut] - interior(carried))
        spread_moment = spread_moment + weight * (
            moment_two[row_cut, col_cut] - interior(moment_two)
        )
    trait_mid = interior(trait_now)
    variance_mid = interior(variance_now)
    denominator = spread_density + PRIOR_WEIGHT
    trait_spread = (spread_carried + PRIOR_WEIGHT * trait_mid) / denominator
    second_spread = (
        spread_moment + PRIOR_WEIGHT * (variance_mid + trait_mid * trait_mid)
    ) / denominator
    variance_spread = second_spread - trait_spread * trait_spread
    offset = trait_spread - interior(optimum_map)
    growth = land_mid * (
        GROWTH_RATE * (1.0 - spread_density) - 0.5 * selection * (offset * offset + variance_spread)
    )
    density_new = spread_density * jnp.exp(growth)
    response = selection * variance_spread
    trait_new = trait_spread - response * offset / (1.0 + response)
    variance_new = variance_spread / (1.0 + response) + MUTATION_INPUT
    return jnp.stack([density_new, trait_new, variance_new])


def adam_update(raw_maps, first_now, second_now, gradient):
    first_new = BETA_FIRST * first_now + (1.0 - BETA_FIRST) * gradient
    second_new = BETA_SECOND * second_now + (1.0 - BETA_SECOND) * gradient * gradient
    first_hat = first_new / (1.0 - BETA_FIRST**ADAM_STEP)
    second_hat = second_new / (1.0 - BETA_SECOND**ADAM_STEP)
    maps_new = raw_maps - LEARN_RATE * first_hat / (jnp.sqrt(second_hat) + ADAM_EPS)
    return (maps_new, first_new, second_new)


def state_halo(fields):
    return extended(fields, (("lx", 1), ("ly", 2)), 2)


def adjoint_halo(adjoint_now):
    return extended(adjoint_now, (("lx", 1), ("ly", 2)), 1)


def shards(
    density,
    trait,
    variance,
    optimum,
    observed,
    obs_step,
    land_code,
    maps,
    first_moment,
    second_moment,
):
    land_frac = land_code.astype(jnp.float32)
    statics = jnp.concatenate([maps, optimum, land_frac[None]], axis=0)
    fields = jnp.concatenate([density, trait, variance], axis=0)
    padded_states = []
    later_states = []
    static_wide = extended(statics, (("lx", 1), ("ly", 2)), 2)
    raw_near = interior(static_wide[0:2])
    optimum_near = interior(static_wide[2])
    land_near = interior(static_wide[3])
    for step_index in range(STEPS):
        padded = state_halo(fields)
        padded_states.append(padded)
        fields = advance(interior(padded), raw_near, optimum_near, land_near)
        later_states.append(fields)
    raw_wide = static_wide[0:2]
    optimum_wide = static_wide[2]
    land_wide = static_wide[3]
    chosen_rows = obs_step[0]

    def forward_wide(field_block, raw_block):
        return advance(field_block, raw_block, optimum_wide, land_wide)

    adjoint_now = jnp.zeros_like(later_states[-1])
    gradient = jnp.zeros(maps.shape, jnp.float32)
    for step_index in reversed(range(STEPS)):
        chosen = (chosen_rows == step_index + 1).astype(jnp.float32)[:, None]
        source = (
            2.0 * LOSS_WEIGHT * chosen * land_frac * (later_states[step_index][0] - observed[0])
        )
        blank = jnp.zeros_like(source)
        adjoint_now = adjoint_now + jnp.stack([source, blank, blank])
        adjoint_wide = adjoint_halo(adjoint_now)
        outputs, pullback = jax.vjp(forward_wide, padded_states[step_index], raw_wide)
        cot_fields, cot_maps = pullback(adjoint_wide)
        adjoint_now = cot_fields[:, 2:-2, 2:-2]
        gradient = gradient + cot_maps[:, 2:-2, 2:-2]
    share = lax.psum_scatter(gradient, "scen", scatter_dimension=1, tiled=True)
    share_rows = share.shape[1]
    row_start = lax.axis_index("scen") * share_rows
    maps_own = lax.dynamic_slice_in_dim(maps, row_start, share_rows, 1)
    first_own = lax.dynamic_slice_in_dim(first_moment, row_start, share_rows, 1)
    second_own = lax.dynamic_slice_in_dim(second_moment, row_start, share_rows, 1)
    maps_part, first_part, second_part = adam_update(maps_own, first_own, second_own, share)
    new_maps, new_first, new_second = (
        lax.all_gather(maps_part, "scen", axis=1, tiled=True),
        lax.all_gather(first_part, "scen", axis=1, tiled=True),
        lax.all_gather(second_part, "scen", axis=1, tiled=True),
    )
    return (new_maps, new_first, new_second)


def solution(mesh):
    in_specs = (
        P("scen", "lx", "ly"),
        P("scen", "lx", "ly"),
        P("scen", "lx", "ly"),
        P("scen", "lx", "ly"),
        P("scen", "lx", "ly"),
        P("scen", "lx"),
        P("lx", "ly"),
        P(None, "lx", "ly"),
        P(None, "lx", "ly"),
        P(None, "lx", "ly"),
    )
    out_specs = (P(None, "lx", "ly"), P(None, "lx", "ly"), P(None, "lx", "ly"))
    return jax.shard_map(shards, mesh=mesh, in_specs=in_specs, out_specs=out_specs, check_vma=False)
```

profile of v0, /device:TPU:32, one launch (start us, length us, event | category | flops | bytes accessed | tf_op | source)
XLA Modules:
  0.0 307.5 jit_solution(4712670643608340800)
XLA Ops:
  7.2 1.0 constant_dynamic-update-slice_fusion.2
  10.3 1.9 collective-permute-start
  12.2 3.6 %collective-permute-start.1 = (f32[3,2,512]{2,1,0:T(2,128)S(1)}, f32[3,2,512]{2,1,0:T(2,128)S(1)}, u32[]{:S(2)}, u32[]{:S(2)}) collective-permute-start(f32[3,2,512]{2,1,0:T(2,128)S(1)} %get-tuple-element.120), channel_id=1, source_target_pairs={{4,0},{8,4},{12,8},{5,1},{9,5},{13,9},{6,2},{10,6},{14,10},{7,3},{... | collective-permute-start | bytes 36872 | tf_op jit(solution)/shard_map/ppermute | solution.py:29
  15.9 1.9 collective-permute-start.4
  17.9 3.6 %collective-permute-start.5 = (f32[4,2,512]{2,1,0:T(2,128)S(1)}, f32[4,2,512]{2,1,0:T(2,128)S(1)}, u32[]{:S(2)}, u32[]{:S(2)}) collective-permute-start(f32[4,2,512]{2,1,0:T(2,128)S(1)} %get-tuple-element.86), channel_id=1, source_target_pairs={{4,0},{8,4},{12,8},{5,1},{9,5},{13,9},{6,2},{10,6},{14,10},{7,3},{... | collective-permute-start | bytes 49160 | tf_op jit(solution)/shard_map/ppermute | solution.py:29
  21.7 5.2 %collective-permute-start.2 = (f32[3,132,2]{2,1,0:T(8,128)S(1)}, f32[3,132,2]{2,1,0:T(8,128)S(1)}, u32[]{:S(2)}, u32[]{:S(2)}) collective-permute-start(f32[3,132,2]{2,1,0:T(8,128)S(1)} %get-tuple-element.109), channel_id=1, source_target_pairs={{0,1},{1,2},{2,3},{4,5},{5,6},{6,7},{8,9},{9,10},{10,11},{12,13},{... | collective-permute-start | bytes 9512 | tf_op jit(solution)/shard_map/ppermute | solution.py:26
  26.9 1.3 collective-permute-start.3
  28.2 6.2 %collective-permute-done.2 = f32[3,132,2]{2,1,0:T(8,128)S(1)} collective-permute-done((f32[3,132,2]{2,1,0:T(8,128)S(1)}, f32[3,132,2]{2,1,0:T(8,128)S(1)}, u32[]{:S(2)}, u32[]{:S(2)}) %collective-permute-start.2) | collective-permute-done | bytes 3200 | tf_op jit(solution)/shard_map/ppermute | solution.py:26
  34.4 3.0 collective-permute-done.3
  38.4 8.1 %collective-permute-start.6 = (f32[4,132,2]{2,1,0:T(8,128)S(1)}, f32[4,132,2]{2,1,0:T(8,128)S(1)}, u32[]{:S(2)}, u32[]{:S(2)}) collective-permute-start(f32[4,132,2]{2,1,0:T(8,128)S(1)} %get-tuple-element.83), channel_id=1, source_target_pairs={{0,1},{1,2},{2,3},{4,5},{5,6},{6,7},{8,9},{9,10},{10,11},{12,13},{... | collective-permute-start | bytes 12680 | tf_op jit(solution)/shard_map/ppermute | solution.py:26
  46.5 1.3 collective-permute-start.7
  48.1 7.9 %collective-permute-done.6 = f32[4,132,2]{2,1,0:T(8,128)S(1)} collective-permute-done((f32[4,132,2]{2,1,0:T(8,128)S(1)}, f32[4,132,2]{2,1,0:T(8,128)S(1)}, u32[]{:S(2)}, u32[]{:S(2)}) %collective-permute-start.6) | collective-permute-done | bytes 4256 | tf_op jit(solution)/shard_map/ppermute | solution.py:26
  56.0 5.7 %collective-permute-done.7 = f32[4,132,2]{2,1,0:T(8,128)S(1)} collective-permute-done((f32[4,132,2]{2,1,0:T(8,128)S(1)}, f32[4,132,2]{2,1,0:T(8,128)S(1)}, u32[]{:S(2)}, u32[]{:S(2)}) %collective-permute-start.7) | collective-permute-done | bytes 4256 | tf_op jit(solution)/shard_map/ppermute | solution.py:29
  63.7 1.1 fusion.111
  65.1 1.9 collective-permute-start.8
  67.1 3.6 %collective-permute-start.9 = (f32[3,2,512]{2,1,0:T(2,128)S(1)}, f32[3,2,512]{2,1,0:T(2,128)S(1)}, u32[]{:S(2)}, u32[]{:S(2)}) collective-permute-start(f32[3,2,512]{2,1,0:T(2,128)S(1)} %get-tuple-element.118), channel_id=1, source_target_pairs={{4,0},{8,4},{12,8},{5,1},{9,5},{13,9},{6,2},{10,6},{14,10},{7,3},{... | collective-permute-start | bytes 36872 | tf_op jit(solution)/shard_map/ppermute | solution.py:29
  70.7 1.4 collective-permute-done.9
  72.2 3.1 collective-permute-start.10
  75.3 1.3 collective-permute-start.11
  76.7 5.9 %collective-permute-done.10 = f32[3,132,2]{2,1,0:T(8,128)S(1)} collective-permute-done((f32[3,132,2]{2,1,0:T(8,128)S(1)}, f32[3,132,2]{2,1,0:T(8,128)S(1)}, u32[]{:S(2)}, u32[]{:S(2)}) %collective-permute-start.10) | collective-permute-done | bytes 3200 | tf_op jit(solution)/shard_map/ppermute | solution.py:26
  82.6 5.3 %collective-permute-done.11 = f32[3,132,2]{2,1,0:T(8,128)S(1)} collective-permute-done((f32[3,132,2]{2,1,0:T(8,128)S(1)}, f32[3,132,2]{2,1,0:T(8,128)S(1)}, u32[]{:S(2)}, u32[]{:S(2)}) %collective-permute-start.11) | collective-permute-done | bytes 3200 | tf_op jit(solution)/shard_map/ppermute | solution.py:29
  89.1 1.4 fusion.109
  90.5 1.9 collective-permute-start.12
  92.4 3.6 %collective-permute-start.13 = (f32[3,1,512]{2,1,0:T(1,128)S(1)}, f32[3,1,512]{2,1,0:T(1,128)S(1)}, u32[]{:S(2)}, u32[]{:S(2)}) collective-permute-start(f32[3,1,512]{2,1,0:T(1,128)S(1)} %get-tuple-element.148), channel_id=1, source_target_pairs={{4,0},{8,4},{12,8},{5,1},{9,5},{13,9},{6,2},{10,6},{14,10},{7,3},{... | collective-permute-start | bytes 18440 | tf_op jit(solution)/shard_map/ppermute | solution.py:29
  96.3 1.1 collective-permute-done.13
  97.5 3.2 %collective-permute-start.14 = (f32[3,130,1]{2,1,0:T(8,128)S(1)}, f32[3,130,1]{2,1,0:T(8,128)S(1)}, u32[]{:S(2)}, u32[]{:S(2)}) collective-permute-start(f32[3,130,1]{2,1,0:T(8,128)S(1)} %get-tuple-element.113), channel_id=1, source_target_pairs={{0,1},{1,2},{2,3},{4,5},{5,6},{6,7},{8,9},{9,10},{10,11},{12,13},{... | collective-permute-start | bytes 4688 | tf_op jit(solution)/shard_map/ppermute | solution.py:26
  100.7 1.5 collective-permute-start.15
  102.3 5.8 %collective-permute-done.14 = f32[3,130,1]{2,1,0:T(8,128)S(1)} collective-permute-done((f32[3,130,1]{2,1,0:T(8,128)S(1)}, f32[3,130,1]{2,1,0:T(8,128)S(1)}, u32[]{:S(2)}, u32[]{:S(2)}) %collective-permute-start.14) | collective-permute-done | bytes 1592 | tf_op jit(solution)/shard_map/ppermute | solution.py:26
  108.0 5.3 %collective-permute-done.15 = f32[3,130,1]{2,1,0:T(8,128)S(1)} collective-permute-done((f32[3,130,1]{2,1,0:T(8,128)S(1)}, f32[3,130,1]{2,1,0:T(8,128)S(1)}, u32[]{:S(2)}, u32[]{:S(2)}) %collective-permute-start.15) | collective-permute-done | bytes 1592 | tf_op jit(solution)/shard_map/ppermute | solution.py:29
  113.8 2.4 add_multiply_fusion.2
  116.2 2.3 add_add_fusion.7
  119.2 1.1 add_bitcast_fusion.1
  120.3 1.1 fusion.3
  121.4 1.0 add_bitcast_fusion
  122.7 1.9 collective-permute-start.16
  124.7 3.6 %collective-permute-start.17 = (f32[3,1,512]{2,1,0:T(1,128)S(1)}, f32[3,1,512]{2,1,0:T(1,128)S(1)}, u32[]{:S(2)}, u32[]{:S(2)}) collective-permute-start(f32[3,1,512]{2,1,0:T(1,128)S(1)} %get-tuple-element.116), channel_id=1, source_target_pairs={{4,0},{8,4},{12,8},{5,1},{9,5},{13,9},{6,2},{10,6},{14,10},{7,3},{... | collective-permute-start | bytes 18440 | tf_op jit(solution)/shard_map/ppermute | solution.py:29
  128.4 1.2 collective-permute-done.17
  129.8 3.1 %collective-permute-start.18 = (f32[3,130,1]{2,1,0:T(8,128)S(1)}, f32[3,130,1]{2,1,0:T(8,128)S(1)}, u32[]{:S(2)}, u32[]{:S(2)}) collective-permute-start(f32[3,130,1]{2,1,0:T(8,128)S(1)} %get-tuple-element.111), channel_id=1, source_target_pairs={{0,1},{1,2},{2,3},{4,5},{5,6},{6,7},{8,9},{9,10},{10,11},{12,13},{... | collective-permute-start | bytes 4688 | tf_op jit(solution)/shard_map/ppermute | solution.py:26
  132.9 1.5 collective-permute-start.19
  134.6 5.7 %collective-permute-done.18 = f32[3,130,1]{2,1,0:T(8,128)S(1)} collective-permute-done((f32[3,130,1]{2,1,0:T(8,128)S(1)}, f32[3,130,1]{2,1,0:T(8,128)S(1)}, u32[]{:S(2)}, u32[]{:S(2)}) %collective-permute-start.18) | collective-permute-done | bytes 1592 | tf_op jit(solution)/shard_map/ppermute | solution.py:26
  140.2 5.3 %collective-permute-done.19 = f32[3,130,1]{2,1,0:T(8,128)S(1)} collective-permute-done((f32[3,130,1]{2,1,0:T(8,128)S(1)}, f32[3,130,1]{2,1,0:T(8,128)S(1)}, u32[]{:S(2)}, u32[]{:S(2)}) %collective-permute-start.19) | collective-permute-done | bytes 1592 | tf_op jit(solution)/shard_map/ppermute | solution.py:29
  146.0 2.0 add_multiply_fusion
  149.1 2.3 add_add_fusion.5
  152.2 1.2 fusion.1
  153.4 75.6 %reduce-scatter.2.cloned.1.call-done = f32[2,8,512]{2,1,0:T(8,128)} async-done(((f32[2,128,512]{2,1,0:T(8,128)}), f32[2,8,512]{2,1,0:T(8,128)}) %reduce-scatter.2.cloned.1.call-update) | async-done | bytes 32784 | tf_op jit(solution)/shard_map/reduce_scatter | solution.py:150
  229.9 23.3 %all_gather.9 = f32[2,128,512]{2,1,0:T(8,128)S(1)} all-gather(f32[2,8,512]{2,1,0:T(8,128)S(1)} %get-tuple-element.7), channel_id=1, replica_groups=mesh['scen'=16,'lx'=4,'ly'=4] {'scen'}, dimensions={1}, use_global_device_ids=true | all-gather | bytes 557056 | tf_op jit(solution)/shard_map/all_gather | solution.py:158
  253.2 22.1 %all_gather.10 = f32[2,128,512]{2,1,0:T(8,128)S(1)} all-gather(f32[2,8,512]{2,1,0:T(8,128)S(1)} %get-tuple-element.8), channel_id=1, replica_groups=mesh['scen'=16,'lx'=4,'ly'=4] {'scen'}, dimensions={1}, use_global_device_ids=true | all-gather | bytes 557056 | tf_op jit(solution)/shard_map/all_gather | solution.py:159
  275.3 23.0 %all_gather.11 = f32[2,128,512]{2,1,0:T(8,128)S(1)} all-gather(f32[2,8,512]{2,1,0:T(8,128)S(1)} %get-tuple-element.9), channel_id=1, replica_groups=mesh['scen'=16,'lx'=4,'ly'=4] {'scen'}, dimensions={1}, use_global_device_ids=true | all-gather | bytes 557056 | tf_op jit(solution)/shard_map/all_gather | solution.py:160
  (61 shorter events, 14.9 us)
Async XLA Ops:
  7.2 8.7 %copy-start.1 = (s32[128,512]{1,0:T(8,128)S(1)}, s32[128,512]{1,0:T(8,128)}, u32[]{:S(2)}) copy-start(s32[128,512]{1,0:T(8,128)} %param.17) | copy-start | bytes 786436
  7.2 8.7 %copy-start.2 = (f32[1,128,512]{2,1,0:T(8,128)S(1)}, f32[1,128,512]{2,1,0:T(8,128)}, u32[]{:S(2)}) copy-start(f32[1,128,512]{2,1,0:T(8,128)} %param.14) | copy-start | bytes 786436
  7.2 8.7 %copy-start = (f32[2,128,512]{2,1,0:T(8,128)S(1)}, f32[2,128,512]{2,1,0:T(8,128)}, u32[]{:S(2)}) copy-start(f32[2,128,512]{2,1,0:T(8,128)} %param.18) | copy-start | bytes 1572868
  7.2 221.9 %reduce-scatter.2.cloned.1.call-start = ((), (), s32[]{:S(2)}) async-start(), calls=%async_computation.1 | async-start | bytes 557056 | tf_op jit(solution)/shard_map/reduce_scatter | solution.py:150
  10.3 11.3 %collective-permute-start = (f32[3,2,512]{2,1,0:T(2,128)S(1)}, f32[3,2,512]{2,1,0:T(2,128)S(1)}, u32[]{:S(2)}, u32[]{:S(2)}) collective-permute-start(f32[3,2,512]{2,1,0:T(2,128)S(1)} %get-tuple-element.119), channel_id=1, source_target_pairs={{0,4},{4,8},{8,12},{1,5},{5,9},{9,13},{2,6},{6,10},{10,14},{3,7},{... | collective-permute-start | bytes 36872 | tf_op jit(solution)/shard_map/ppermute | solution.py:26
  12.2 16.0 %copy-start.4 = (s32[1,128]{1,0:T(1,128)S(1)}, s32[1,128]{1,0:T(1,128)}, u32[]{:S(2)}) copy-start(s32[1,128]{1,0:T(1,128)} %param.16) | copy-start | bytes 1540
  12.2 9.3 %collective-permute-start.1 = (f32[3,2,512]{2,1,0:T(2,128)S(1)}, f32[3,2,512]{2,1,0:T(2,128)S(1)}, u32[]{:S(2)}, u32[]{:S(2)}) collective-permute-start(f32[3,2,512]{2,1,0:T(2,128)S(1)} %get-tuple-element.120), channel_id=1, source_target_pairs={{4,0},{8,4},{12,8},{5,1},{9,5},{13,9},{6,2},{10,6},{14,10},{7,3},{... | collective-permute-start | bytes 36872 | tf_op jit(solution)/shard_map/ppermute | solution.py:29
  15.9 22.3 %collective-permute-start.4 = (f32[4,2,512]{2,1,0:T(2,128)S(1)}, f32[4,2,512]{2,1,0:T(2,128)S(1)}, u32[]{:S(2)}, u32[]{:S(2)}) collective-permute-start(f32[4,2,512]{2,1,0:T(2,128)S(1)} %get-tuple-element.85), channel_id=1, source_target_pairs={{0,4},{4,8},{8,12},{1,5},{5,9},{9,13},{2,6},{6,10},{10,14},{3,7},{... | collective-permute-start | bytes 49160 | tf_op jit(solution)/shard_map/ppermute | solution.py:26
  17.9 20.3 %collective-permute-start.5 = (f32[4,2,512]{2,1,0:T(2,128)S(1)}, f32[4,2,512]{2,1,0:T(2,128)S(1)}, u32[]{:S(2)}, u32[]{:S(2)}) collective-permute-start(f32[4,2,512]{2,1,0:T(2,128)S(1)} %get-tuple-element.86), channel_id=1, source_target_pairs={{4,0},{8,4},{12,8},{5,1},{9,5},{13,9},{6,2},{10,6},{14,10},{7,3},{... | collective-permute-start | bytes 49160 | tf_op jit(solution)/shard_map/ppermute | solution.py:29
  21.7 12.7 %collective-permute-start.2 = (f32[3,132,2]{2,1,0:T(8,128)S(1)}, f32[3,132,2]{2,1,0:T(8,128)S(1)}, u32[]{:S(2)}, u32[]{:S(2)}) collective-permute-start(f32[3,132,2]{2,1,0:T(8,128)S(1)} %get-tuple-element.109), channel_id=1, source_target_pairs={{0,1},{1,2},{2,3},{4,5},{5,6},{6,7},{8,9},{9,10},{10,11},{12,13},{... | collective-permute-start | bytes 9512 | tf_op jit(solution)/shard_map/ppermute | solution.py:26
  26.9 10.5 %collective-permute-start.3 = (f32[3,132,2]{2,1,0:T(8,128)S(1)}, f32[3,132,2]{2,1,0:T(8,128)S(1)}, u32[]{:S(2)}, u32[]{:S(2)}) collective-permute-start(f32[3,132,2]{2,1,0:T(8,128)S(1)} %get-tuple-element.110), channel_id=1, source_target_pairs={{1,0},{2,1},{3,2},{5,4},{6,5},{7,6},{9,8},{10,9},{11,10},{13,12},{... | collective-permute-start | bytes 9512 | tf_op jit(solution)/shard_map/ppermute | solution.py:29
  38.4 17.6 %collective-permute-start.6 = (f32[4,132,2]{2,1,0:T(8,128)S(1)}, f32[4,132,2]{2,1,0:T(8,128)S(1)}, u32[]{:S(2)}, u32[]{:S(2)}) collective-permute-start(f32[4,132,2]{2,1,0:T(8,128)S(1)} %get-tuple-element.83), channel_id=1, source_target_pairs={{0,1},{1,2},{2,3},{4,5},{5,6},{6,7},{8,9},{9,10},{10,11},{12,13},{... | collective-permute-start | bytes 12680 | tf_op jit(solution)/shard_map/ppermute | solution.py:26
  46.5 15.3 %collective-permute-start.7 = (f32[4,132,2]{2,1,0:T(8,128)S(1)}, f32[4,132,2]{2,1,0:T(8,128)S(1)}, u32[]{:S(2)}, u32[]{:S(2)}) collective-permute-start(f32[4,132,2]{2,1,0:T(8,128)S(1)} %get-tuple-element.84), channel_id=1, source_target_pairs={{1,0},{2,1},{3,2},{5,4},{6,5},{7,6},{9,8},{10,9},{11,10},{13,12},{... | collective-permute-start | bytes 12680 | tf_op jit(solution)/shard_map/ppermute | solution.py:29
  62.7 1.0 copy-start.3
  65.1 5.6 %collective-permute-start.8 = (f32[3,2,512]{2,1,0:T(2,128)S(1)}, f32[3,2,512]{2,1,0:T(2,128)S(1)}, u32[]{:S(2)}, u32[]{:S(2)}) collective-permute-start(f32[3,2,512]{2,1,0:T(2,128)S(1)} %get-tuple-element.117), channel_id=1, source_target_pairs={{0,4},{4,8},{8,12},{1,5},{5,9},{9,13},{2,6},{6,10},{10,14},{3,7},{... | collective-permute-start | bytes 36872 | tf_op jit(solution)/shard_map/ppermute | solution.py:26
  67.1 5.0 %collective-permute-start.9 = (f32[3,2,512]{2,1,0:T(2,128)S(1)}, f32[3,2,512]{2,1,0:T(2,128)S(1)}, u32[]{:S(2)}, u32[]{:S(2)}) collective-permute-start(f32[3,2,512]{2,1,0:T(2,128)S(1)} %get-tuple-element.118), channel_id=1, source_target_pairs={{4,0},{8,4},{12,8},{5,1},{9,5},{13,9},{6,2},{10,6},{14,10},{7,3},{... | collective-permute-start | bytes 36872 | tf_op jit(solution)/shard_map/ppermute | solution.py:29
  72.2 10.4 %collective-permute-start.10 = (f32[3,132,2]{2,1,0:T(8,128)S(1)}, f32[3,132,2]{2,1,0:T(8,128)S(1)}, u32[]{:S(2)}, u32[]{:S(2)}) collective-permute-start(f32[3,132,2]{2,1,0:T(8,128)S(1)} %get-tuple-element.107), channel_id=1, source_target_pairs={{0,1},{1,2},{2,3},{4,5},{5,6},{6,7},{8,9},{9,10},{10,11},{12,13},{... | collective-permute-start | bytes 9512 | tf_op jit(solution)/shard_map/ppermute | solution.py:26
  75.3 12.6 %collective-permute-start.11 = (f32[3,132,2]{2,1,0:T(8,128)S(1)}, f32[3,132,2]{2,1,0:T(8,128)S(1)}, u32[]{:S(2)}, u32[]{:S(2)}) collective-permute-start(f32[3,132,2]{2,1,0:T(8,128)S(1)} %get-tuple-element.108), channel_id=1, source_target_pairs={{1,0},{2,1},{3,2},{5,4},{6,5},{7,6},{9,8},{10,9},{11,10},{13,12},{... | collective-permute-start | bytes 9512 | tf_op jit(solution)/shard_map/ppermute | solution.py:29
  90.5 5.8 %collective-permute-start.12 = (f32[3,1,512]{2,1,0:T(1,128)S(1)}, f32[3,1,512]{2,1,0:T(1,128)S(1)}, u32[]{:S(2)}, u32[]{:S(2)}) collective-permute-start(f32[3,1,512]{2,1,0:T(1,128)S(1)} %get-tuple-element.147), channel_id=1, source_target_pairs={{0,4},{4,8},{8,12},{1,5},{5,9},{9,13},{2,6},{6,10},{10,14},{3,7},{... | collective-permute-start | bytes 18440 | tf_op jit(solution)/shard_map/ppermute | solution.py:26
  92.4 5.0 %collective-permute-start.13 = (f32[3,1,512]{2,1,0:T(1,128)S(1)}, f32[3,1,512]{2,1,0:T(1,128)S(1)}, u32[]{:S(2)}, u32[]{:S(2)}) collective-permute-start(f32[3,1,512]{2,1,0:T(1,128)S(1)} %get-tuple-element.148), channel_id=1, source_target_pairs={{4,0},{8,4},{12,8},{5,1},{9,5},{13,9},{6,2},{10,6},{14,10},{7,3},{... | collective-permute-start | bytes 18440 | tf_op jit(solution)/shard_map/ppermute | solution.py:29
  97.5 10.5 %collective-permute-start.14 = (f32[3,130,1]{2,1,0:T(8,128)S(1)}, f32[3,130,1]{2,1,0:T(8,128)S(1)}, u32[]{:S(2)}, u32[]{:S(2)}) collective-permute-start(f32[3,130,1]{2,1,0:T(8,128)S(1)} %get-tuple-element.113), channel_id=1, source_target_pairs={{0,1},{1,2},{2,3},{4,5},{5,6},{6,7},{8,9},{9,10},{10,11},{12,13},{... | collective-permute-start | bytes 4688 | tf_op jit(solution)/shard_map/ppermute | solution.py:26
  100.7 12.7 %collective-permute-start.15 = (f32[3,130,1]{2,1,0:T(8,128)S(1)}, f32[3,130,1]{2,1,0:T(8,128)S(1)}, u32[]{:S(2)}, u32[]{:S(2)}) collective-permute-start(f32[3,130,1]{2,1,0:T(8,128)S(1)} %get-tuple-element.114), channel_id=1, source_target_pairs={{1,0},{2,1},{3,2},{5,4},{6,5},{7,6},{9,8},{10,9},{11,10},{13,12},{... | collective-permute-start | bytes 4688 | tf_op jit(solution)/shard_map/ppermute | solution.py:29
  122.7 5.7 %collective-permute-start.16 = (f32[3,1,512]{2,1,0:T(1,128)S(1)}, f32[3,1,512]{2,1,0:T(1,128)S(1)}, u32[]{:S(2)}, u32[]{:S(2)}) collective-permute-start(f32[3,1,512]{2,1,0:T(1,128)S(1)} %get-tuple-element.115), channel_id=1, source_target_pairs={{0,4},{4,8},{8,12},{1,5},{5,9},{9,13},{2,6},{6,10},{10,14},{3,7},{... | collective-permute-start | bytes 18440 | tf_op jit(solution)/shard_map/ppermute | solution.py:26
  124.7 5.0 %collective-permute-start.17 = (f32[3,1,512]{2,1,0:T(1,128)S(1)}, f32[3,1,512]{2,1,0:T(1,128)S(1)}, u32[]{:S(2)}, u32[]{:S(2)}) collective-permute-start(f32[3,1,512]{2,1,0:T(1,128)S(1)} %get-tuple-element.116), channel_id=1, source_target_pairs={{4,0},{8,4},{12,8},{5,1},{9,5},{13,9},{6,2},{10,6},{14,10},{7,3},{... | collective-permute-start | bytes 18440 | tf_op jit(solution)/shard_map/ppermute | solution.py:29
  129.8 10.5 %collective-permute-start.18 = (f32[3,130,1]{2,1,0:T(8,128)S(1)}, f32[3,130,1]{2,1,0:T(8,128)S(1)}, u32[]{:S(2)}, u32[]{:S(2)}) collective-permute-start(f32[3,130,1]{2,1,0:T(8,128)S(1)} %get-tuple-element.111), channel_id=1, source_target_pairs={{0,1},{1,2},{2,3},{4,5},{5,6},{6,7},{8,9},{9,10},{10,11},{12,13},{... | collective-permute-start | bytes 4688 | tf_op jit(solution)/shard_map/ppermute | solution.py:26
  132.9 12.7 %collective-permute-start.19 = (f32[3,130,1]{2,1,0:T(8,128)S(1)}, f32[3,130,1]{2,1,0:T(8,128)S(1)}, u32[]{:S(2)}, u32[]{:S(2)}) collective-permute-start(f32[3,130,1]{2,1,0:T(8,128)S(1)} %get-tuple-element.112), channel_id=1, source_target_pairs={{1,0},{2,1},{3,2},{5,4},{6,5},{7,6},{9,8},{10,9},{11,10},{13,12},{... | collective-permute-start | bytes 4688 | tf_op jit(solution)/shard_map/ppermute | solution.py:29
Sparse Core Ops, SparseCore 0:
  153.5 75.4 reduce-scatter.1
where the time goes:
time: 308 us
  waiting for transfers between devices  135 us (44%)
  blocking collectives  68.4 us (22%)
  starting transfers between devices  57.4 us (19%)
  other arithmetic  25 us (8%)
  between operations  14.6 us (5%)
  local copies, waits for them, and re-layouts  6.75 us (2%)
    reduce_scatter x1, waiting for transfers between devices, shards(): share = lax.psum_scatter(gradient, 'scen', scatter_dimension=1, tiled=True)  75.6 us
    ppermute x10, starting transfers between devices, extended(): lax.ppermute(lax.slice_in_dim(block, block.shape[dim] - width, None, axis...  32.2 us
    ppermute x10, waiting for transfers between devices, extended(): lax.ppermute(lax.slice_in_dim(block, block.shape[dim] - width, None, axis...  31.4 us
    ppermute x10, waiting for transfers between devices, extended(): lax.ppermute(lax.slice_in_dim(block, 0, width, axis=dim), axis, backward)  28.4 us
    ppermute x10, starting transfers between devices, extended(): lax.ppermute(lax.slice_in_dim(block, 0, width, axis=dim), axis, backward)  25.1 us
    all_gather x1, blocking collectives, shards(): lax.all_gather(maps_part, 'scen', axis=1, tiled=True)  23.3 us
    all_gather x1, blocking collectives, shards(): lax.all_gather(second_part, 'scen', axis=1, tiled=True)  23 us
    all_gather x1, blocking collectives, shards(): lax.all_gather(first_part, 'scen', axis=1, tiled=True)  22.1 us
  transfers between devices with their start and end apart: 21, of which 14 were waited for; matrix products, arithmetic and copies ran while one was open for 1% of the time, Pallas kernels for 0%

commit v1 on v0

v1 whole, which is shorter than its diff:
```python
import functools

import jax
import jax.numpy as jnp
from jax import lax
from jax.experimental import pallas as pl
from jax.experimental.pallas import tpu as pltpu
from jax.sharding import PartitionSpec as P

ADAM_STEP = 10
REACH_MAX = 0.2
PRIOR = 0.1
GROWTH = 0.5
MUTATION = 0.02
LEARN_RATE = 0.01
BETA_FIRST = 0.9
BETA_SECOND = 0.999
ADAM_EPS = 1e-08
LOSS_WEIGHT = 2.0

MESH = pl.DeviceIdType.MESH
SUB, LANE = 8, 128
BANDS = 4
OFF = 16
DENS, TRAIT, VAR, OPT, OBS, MAP0, MAP1, LAND = range(8)
SIDES = [(-1, -1), (-1, 0), (-1, 1), (0, -1), (0, 1), (1, -1), (1, 0), (1, 1)]
NAMES = (
    "n0", "q0", "m0", "s0", "rho", "lnd", "sel", "wx",
    "wy", "n1", "q1", "m1", "z1", "s1", "e1", "r1",
    "zs1", "ss1", "u1", "fxn", "fxq", "fxm", "gxn", "gxq",
    "gxm", "ln", "lq", "lm", "kn", "kq", "km", "ds",
    "gx", "gy", "hy", "fac0", "fac1",
)
PLANE = {name: index for index, name in enumerate(NAMES)}


def kernel(
    sizes,
    dens,
    trait,
    var,
    opt,
    obs,
    ostep,
    land,
    maps,
    first,
    second,
    o_maps,
    o_first,
    o_second,
    raw,
    rawl,
    own_k,
    up_k,
    down_k,
    krow,
    colsend,
    colrx,
    cornrx,
    square,
    mom,
    planes,
    gsend,
    rrx,
    gfull,
    outs,
    load_sem,
    row_send,
    row_recv,
    col_send,
    col_recv,
    rs_send,
    rs_recv,
    ag_send,
    ag_recv,
    out_sem,
):
    ns, nx, ny, rows, cols = sizes
    tiles = cols // LANE
    wide = tiles + 1
    blocks = rows // SUB
    per_band = blocks // BANDS
    pieces = per_band * tiles // ns
    me_s, me_x, me_y = (lax.axis_index(name) for name in ("scen", "lx", "ly"))
    top, bottom = me_x == 0, me_x == nx - 1
    left, right = me_y == 0, me_y == ny - 1
    lane = lax.broadcasted_iota(jnp.int32, (SUB, LANE), 1)
    sub = lax.broadcasted_iota(jnp.int32, (SUB, LANE), 0)

    def there(dx, dy):
        ok = jnp.bool_(True)
        if dx:
            ok = jnp.logical_not(top if dx < 0 else bottom)
        if dy:
            oky = jnp.logical_not(left if dy < 0 else right)
            ok = jnp.logical_and(ok, oky) if dx else oky
        return ok

    def target(dx, dy):
        return {"lx": me_x + dx, "ly": me_y + dy}

    body = pl.ds(SUB, rows)
    loads = []
    for slot, ref in enumerate((dens, trait, var, opt, obs)):
        loads.append((ref.at[0], raw.at[slot, body, pl.ds(0, cols)]))
    for slot in range(2):
        loads.append((maps.at[slot], raw.at[MAP0 + slot, body, pl.ds(0, cols)]))
    loads.append((land, rawl.at[body, pl.ds(0, cols)]))
    loads.append((ostep, own_k))
    loads.append((first, mom.at[0]))
    loads.append((second, mom.at[1]))
    loads = [
        pltpu.make_async_copy(src, dst, load_sem.at[slot])
        for slot, (src, dst) in enumerate(loads)
    ]
    for copy in loads:
        copy.start()

    barrier = pltpu.get_barrier_semaphore()

    def greet(step, carry):
        pl.semaphore_signal(
            barrier, inc=1, device_id={"scen": lax.rem(me_s + step, ns)}, device_id_type=MESH
        )
        return carry

    lax.fori_loop(1, ns, greet, 0)
    for dx, dy in SIDES:

        @pl.when(there(dx, dy))
        def _(dx=dx, dy=dy):
            pl.semaphore_signal(barrier, inc=1, device_id=target(dx, dy), device_id_type=MESH)

    over_x = jnp.where(top, 0, 1) + jnp.where(bottom, 0, 1)
    over_y = jnp.where(left, 0, 1) + jnp.where(right, 0, 1)
    pl.semaphore_wait(barrier, ns - 1 + (over_x + 1) * (over_y + 1) - 1)

    def row_copies(dx):
        edge = pl.ds(0, SUB) if dx < 0 else pl.ds(rows - SUB, SUB)
        halo = pl.ds(rows + SUB, SUB) if dx < 0 else pl.ds(0, SUB)
        across = pl.ds(0, cols)
        pairs = [
            (ref.at[0, edge, :], raw.at[slot, halo, across])
            for slot, ref in enumerate((dens, trait, var, opt, obs))
        ]
        pairs.append((maps.at[:, edge, :], raw.at[pl.ds(MAP0, 2), halo, across]))
        pairs.append((land.at[edge, :], rawl.at[halo, across]))
        pairs.append((ostep, down_k if dx < 0 else up_k))
        way = 0 if dx < 0 else 1
        return [
            pltpu.make_async_remote_copy(
                src_ref=src,
                dst_ref=dst,
                send_sem=row_send.at[way, slot],
                recv_sem=row_recv.at[way, slot],
                device_id=target(dx, 0),
                device_id_type=MESH,
            )
            for slot, (src, dst) in enumerate(pairs)
        ]

    for dx in (-1, 1):

        @pl.when(there(dx, 0))
        def _(dx=dx):
            for copy in row_copies(dx):
                copy.start()

    for copy in loads[:9]:
        copy.wait()

    def field(slot, rws, cls):
        if slot == LAND:
            return rawl[rws, cls].astype(jnp.float32)
        return raw[slot, rws, cls]

    def pack(block, carry):
        rws = pl.ds(pl.multiple_of(SUB + block * SUB, SUB), SUB)
        packed = jnp.zeros((SUB, LANE), jnp.float32)
        for slot in range(8):
            pair = jnp.where(
                lane < LANE // 2,
                field(slot, rws, pl.ds(0, LANE)),
                field(slot, rws, pl.ds(cols - LANE, LANE)),
            )
            turned = pltpu.roll(pair, 8 * slot + 4, 1)
            packed = jnp.where(lane // 8 == slot, turned, packed)
        square[pl.ds(pl.multiple_of(block * SUB, SUB), SUB), :] = packed
        return carry

    lax.fori_loop(0, blocks, pack, 0)
    turned = jnp.transpose(square[...])
    corner = jnp.zeros((SUB, LANE), jnp.float32)
    for slot in range(8):
        part = turned[8 * slot : 8 * slot + 8, :]
        corner = jnp.where(lane // 8 == slot, pltpu.roll(part, 8 * slot + 4, 1), corner)
    colsend[0:64, :] = turned[0:64, :]
    colsend[64:72, :] = corner

    def col_copy(dx, dy):
        index = SIDES.index((dx, dy))
        came = SIDES.index((-dx, -dy))
        if dx == 0:
            src, dst = colsend.at[0:64, :], colrx.at[0 if dy > 0 else 1]
        else:
            src, dst = colsend.at[64:72, :], cornrx.at[came]
        return pltpu.make_async_remote_copy(
            src_ref=src,
            dst_ref=dst,
            send_sem=col_send.at[index],
            recv_sem=col_recv.at[came],
            device_id=target(dx, dy),
            device_id_type=MESH,
        )

    col_sides = [side for side in SIDES if side[1]]
    for dx, dy in col_sides:

        @pl.when(there(dx, dy))
        def _(dx=dx, dy=dy):
            col_copy(dx, dy).start()

    def prepare(block, lanes):
        src = pl.ds(pl.multiple_of(block * SUB, SUB), SUB)
        dst = pl.ds(pl.multiple_of(block * SUB + OFF - SUB, SUB), SUB)
        for tile in lanes:
            cls = pl.ds(tile * LANE, LANE)
            n, z, v = raw[DENS, src, cls], raw[TRAIT, src, cls], raw[VAR, src, cls]
            second_moment = v + z * z

            def put(name, value):
                planes[PLANE[name], tile, dst, :] = value

            put("n0", n)
            put("q0", n * z)
            put("s0", second_moment)
            put("m0", n * second_moment)
            put("lnd", rawl[src, cls].astype(jnp.float32))
            share = 1.0 / (1.0 + jnp.exp(-raw[MAP0, src, cls]))
            rho = (0.5 * REACH_MAX) * share
            put("rho", rho)
            x = raw[MAP1, src, cls]
            small = jnp.exp(-jnp.abs(x))
            put("sel", jnp.maximum(x, 0.0) + jnp.log1p(small))
            if tile < tiles:
                put("fac0", rho * (1.0 - share))
                put("fac1", jnp.where(x >= 0.0, 1.0, small) / (1.0 + small))

    def prepare_own(block, carry):
        prepare(block, range(tiles))
        return carry

    lax.fori_loop(1, blocks + 1, prepare_own, 0)

    zero = jnp.zeros((SUB, LANE), jnp.float32)
    for dx, halo, kref in ((-1, 0, up_k), (1, rows + SUB, down_k)):

        @pl.when(there(dx, 0))
        def _(dx=dx):
            for copy in row_copies(-dx):
                copy.wait_recv()

        @pl.when(jnp.logical_not(there(dx, 0)))
        def _(halo=halo, kref=kref):
            for tile in range(tiles):
                cls = pl.ds(tile * LANE, LANE)
                for slot in range(7):
                    raw[slot, pl.ds(halo, SUB), cls] = zero
                rawl[pl.ds(halo, SUB), cls] = jnp.zeros((SUB, LANE), jnp.int32)
            kref[...] = jnp.zeros_like(kref)

    for dx, dy in col_sides:

        @pl.when(there(dx, dy))
        def _(dx=dx, dy=dy):
            col_copy(-dx, -dy).wait_recv()

        @pl.when(jnp.logical_not(there(dx, dy)))
        def _(dx=dx, dy=dy):
            if dx == 0:
                colrx[0 if dy < 0 else 1] = jnp.zeros((64, LANE), jnp.float32)
            else:
                cornrx[SIDES.index((dx, dy))] = zero

    for slot in range(8):
        part = pl.ds(8 * slot, 8)
        square[part, :] = jnp.where(sub < 4, colrx[0, part, :], colrx[1, part, :])
    upper = lax.rem(lane, 8) < 4
    square[64:72, :] = jnp.where(
        sub < 4,
        jnp.where(upper, cornrx[SIDES.index((-1, -1))], cornrx[SIDES.index((1, -1))]),
        jnp.where(upper, cornrx[SIDES.index((-1, 1))], cornrx[SIDES.index((1, 1))]),
    )

    def steps_of(ref):
        return jnp.broadcast_to(ref[...], (SUB, LANE)).astype(jnp.float32)

    square[72:80, :] = jnp.where(
        sub == 0,
        steps_of(own_k),
        jnp.where(sub == 1, steps_of(up_k), jnp.where(sub == 2, steps_of(down_k), 0.0)),
    )
    square[80:128, :] = jnp.zeros((48, LANE), jnp.float32)
    square[...] = jnp.transpose(square[...])

    halo_lanes = pl.ds(cols, LANE)

    def put_halo(slot, rws, value):
        if slot == LAND:
            rawl[rws, halo_lanes] = value.astype(jnp.int32)
        else:
            raw[slot, rws, halo_lanes] = value

    def unpack(block, carry):
        got = square[pl.ds(pl.multiple_of(block * SUB, SUB), SUB), :]
        rws = pl.ds(pl.multiple_of(SUB + block * SUB, SUB), SUB)
        for slot in range(8):
            put_halo(slot, rws, pltpu.roll(got, LANE - (8 * slot + 4), 1))
        krow[rws, :] = jnp.broadcast_to(got[:, 72:73], (SUB, LANE))
        return carry

    lax.fori_loop(0, blocks, unpack, 0)
    for slot in range(8):
        got = pltpu.roll(square[8 * slot : 8 * slot + 8, :], LANE - 68, 1)
        got = pltpu.roll(got, 4, 0)
        put_halo(slot, pl.ds(0, SUB), got)
        put_halo(slot, pl.ds(rows + SUB, SUB), got)
    krow[0:SUB, :] = jnp.broadcast_to(square[rows - SUB : rows, 73:74], (SUB, LANE))
    krow[rows + SUB : rows + 2 * SUB, :] = jnp.broadcast_to(square[0:SUB, 74:75], (SUB, LANE))

    def prepare_side(block, carry):
        prepare(block, (tiles,))
        return carry

    lax.fori_loop(0, blocks + 2, prepare_side, 0)
    prepare(0, range(tiles))
    prepare(blocks + 1, range(tiles))

    def east(values):
        turned = [pltpu.roll(value, LANE - 1, 1) for value in values]
        return [
            jnp.where(lane == LANE - 1, turned[(tile + 1) % wide], turned[tile])
            for tile in range(wide)
        ]

    def west(values):
        turned = [pltpu.roll(value, 1, 1) for value in values]
        return [
            jnp.where(lane == 0, turned[(tile - 1) % wide], turned[tile])
            for tile in range(wide)
        ]

    def getter(row):
        def get(name, shift=0):
            if shift == 0:
                rws = pl.ds(pl.multiple_of(row, SUB), SUB)
            else:
                rws = pl.ds(row + shift, SUB)
            return [planes[PLANE[name], tile, rws, :] for tile in range(wide)]

        def put(name, values):
            rws = pl.ds(pl.multiple_of(row, SUB), SUB)
            for tile, value in enumerate(values):
                planes[PLANE[name], tile, rws, :] = value

        def get_raw(slot):
            rws = pl.ds(pl.multiple_of(row - SUB, SUB), SUB)
            return [raw[slot, rws, tile * LANE : (tile + 1) * LANE] for tile in range(wide)]

        return get, put, get_raw

    def spread(get, name, wx, wy, wyn, keep=None, put=None):
        here = get(name)
        fx = [e - c for e, c in zip(east(here), here)]
        if keep is not None:
            put(keep, fx)
        flow = [w * f for w, f in zip(wx, fx)]
        back = west(flow)
        result = [c + (f - b) for c, f, b in zip(here, flow, back)]
        south, north = get(name, 1), get(name, -1)
        result = [
            a + (w * (s - c) + v * (n - c))
            for a, w, s, c, v, n in zip(result, wy, south, here, wyn, north)
        ]
        return result, fx, [s - c for s, c in zip(south, here)]

    def pass_one(block, carry):
        row = block * SUB
        get, put, get_raw = getter(row)
        rho, lnd = get("rho"), get("lnd")
        rho_e, lnd_e = east(rho), east(lnd)
        wx = [(a + b) * (c * d) for a, b, c, d in zip(rho, rho_e, lnd, lnd_e)]
        rho_s, lnd_s = get("rho", 1), get("lnd", 1)
        wy = [(a + b) * (c * d) for a, b, c, d in zip(rho, rho_s, lnd, lnd_s)]
        rho_n, lnd_n = get("rho", -1), get("lnd", -1)
        wyn = [(a + b) * (c * d) for a, b, c, d in zip(rho, rho_n, lnd, lnd_n)]
        put("wx", wx)
        put("wy", wy)
        ns_, _, _ = spread(get, "n0", wx, wy, wyn, "fxn", put)
        qs_, _, _ = spread(get, "q0", wx, wy, wyn, "fxq", put)
        ms_, _, _ = spread(get, "m0", wx, wy, wyn, "fxm", put)
        z, s0, sel, optimum = get_raw(TRAIT), get("s0"), get("sel"), get_raw(OPT)
        rws = pl.ds(pl.multiple_of(row, SUB), SUB)
        for tile in range(wide):

            def one(name, value, tile=tile):
                planes[PLANE[name], tile, rws, :] = value

            recip = 1.0 / (ns_[tile] + PRIOR)
            zs = (qs_[tile] + PRIOR * z[tile]) * recip
            ss = (ms_[tile] + PRIOR * s0[tile]) * recip
            vs = ss - zs * zs
            d = zs - optimum[tile]
            growth = lnd[tile] * (
                GROWTH - GROWTH * ns_[tile] - 0.5 * sel[tile] * (d * d + vs)
            )
            grown = jnp.exp(growth)
            n1 = ns_[tile] * grown
            response = sel[tile] * vs
            u = 1.0 / (1.0 + response)
            z1 = zs - response * u * d
            s1 = vs * u + MUTATION + z1 * z1
            one("e1", grown)
            one("r1", recip)
            one("zs1", zs)
            one("ss1", ss)
            one("u1", u)
            one("n1", n1)
            one("z1", z1)
            one("s1", s1)
            one("q1", n1 * z1)
            one("m1", n1 * s1)
        return carry

    def pass_two(block, carry):
        row = block * SUB
        get, put, get_raw = getter(row)
        wx, wy, wyn = get("wx"), get("wy"), get("wy", -1)
        ns_, _, _ = spread(get, "n1", wx, wy, wyn, "gxn", put)
        qs_, _, _ = spread(get, "q1", wx, wy, wyn, "gxq", put)
        ms_, _, _ = spread(get, "m1", wx, wy, wyn, "gxm", put)
        z, s1, sel, lnd = get("z1"), get("s1"), get("sel"), get("lnd")
        optimum, observed = get_raw(OPT), get_raw(OBS)
        rws = pl.ds(pl.multiple_of(row, SUB), SUB)
        chosen = krow[pl.ds(pl.multiple_of(row - SUB, SUB), SUB), :]
        loss = jnp.where(chosen == 2.0, 2.0 * LOSS_WEIGHT, 0.0)
        for tile in range(wide):

            def one(name, value, tile=tile):
                planes[PLANE[name], tile, rws, :] = value

            recip = 1.0 / (ns_[tile] + PRIOR)
            zs = (qs_[tile] + PRIOR * z[tile]) * recip
            ss = (ms_[tile] + PRIOR * s1[tile]) * recip
            o = optimum[tile]
            phi = ss + o * (o - 2.0 * zs)
            growth = lnd[tile] * (GROWTH - GROWTH * ns_[tile] - 0.5 * sel[tile] * phi)
            grown = jnp.exp(growth)
            n2 = ns_[tile] * grown
            a = (loss * lnd[tile]) * (n2 - observed[tile])
            g = a * n2
            gs = g * sel[tile] * recip
            lq = gs * o
            lm = -0.5 * gs
            one("lq", lq)
            one("lm", lm)
            one("ln", a * grown - 0.5 * g - (zs * lq + ss * lm))
            one("ds", -0.5 * g * phi)
        return carry

    def pass_three(block, carry):
        row = block * SUB
        get, put, get_raw = getter(row)
        wx, wy, wyn = get("wx"), get("wy"), get("wy", -1)
        spreads = []
        gx = gy = None
        for name, state, kept in (("ln", "n1", "gxn"), ("lq", "q1", "gxq"), ("lm", "m1", "gxm")):
            result, fx, fy = spread(get, name, wx, wy, wyn)
            spreads.append(result)
            here, south = get(state), get(state, 1)
            px = [a * b for a, b in zip(fx, get(kept))]
            py = [a * (s - c) for a, s, c in zip(fy, south, here)]
            gx = px if gx is None else [a + b for a, b in zip(gx, px)]
            gy = py if gy is None else [a + b for a, b in zip(gy, py)]
        put("gx", gx)
        put("gy", gy)
        mu_n, mu_q, mu_m = spreads
        names = ("n1", "z1", "s1", "e1", "r1", "zs1", "ss1", "u1", "sel", "lnd", "lq", "lm", "ds")
        vals = {name: get(name) for name in names}
        optimum, observed = get_raw(OPT), get_raw(OBS)
        rws = pl.ds(pl.multiple_of(row, SUB), SUB)
        chosen = krow[pl.ds(pl.multiple_of(row - SUB, SUB), SUB), :]
        loss = jnp.where(chosen == 1.0, 2.0 * LOSS_WEIGHT, 0.0)
        for tile in range(wide):

            def one(name, value, tile=tile):
                planes[PLANE[name], tile, rws, :] = value

            n1, z1, s1, grown, recip, zs, ss, u, sel, lnd, lq, lm, ds = (
                vals[name][tile] for name in names
            )
            c = mu_m[tile] * n1 + PRIOR * lm
            b = mu_q[tile] * n1 + PRIOR * lq + 2.0 * z1 * c
            a = (loss * lnd) * (n1 - observed[tile]) + (
                mu_n[tile] + mu_q[tile] * z1 + mu_m[tile] * s1
            )
            d = zs - optimum[tile]
            vs = ss - zs * zs
            g = a * n1 * lnd
            phi = d * d + vs
            dr = -(u * u) * (b * d + c * vs)
            gs = g * sel
            dd = -(gs * d + b * (1.0 - u))
            dv = c * u + dr * sel - 0.5 * gs
            kq = recip * (b + dd - 2.0 * zs * dv)
            km = recip * dv
            one("kq", kq)
            one("km", km)
            one("kn", a * grown - 0.5 * g - (zs * kq + ss * km))
            one("ds", ds + (dr * vs - 0.5 * g * phi))
        return carry

    def pass_four(block, carry):
        row = block * SUB
        get, put, _ = getter(row)
        gx, gy = get("gx"), get("gy")
        for name, state, kept in (("kn", "n0", "fxn"), ("kq", "q0", "fxq"), ("km", "m0", "fxm")):
            here = get(name)
            fx = get(kept)
            gx = [a + (e - c) * f for a, e, c, f in zip(gx, east(here), here, fx)]
            old = get(state)
            gy = [
                a + (s - c) * (t - o)
                for a, s, c, t, o in zip(gy, get(name, 1), here, get(state, 1), old)
            ]
        lnd, lnd_s = get("lnd"), get("lnd", 1)
        lnd_e = east(lnd)
        hx = [g * (a * b) for g, a, b in zip(gx, lnd, lnd_e)]
        hy = [g * (a * b) for g, a, b in zip(gy, lnd, lnd_s)]
        put("hy", hy)
        total = [a + b + c + d for a, b, c, d in zip(hx, west(hx), hy, get("hy", -1))]
        ds = get("ds")
        rws = pl.ds(pl.multiple_of(row, SUB), SUB)
        for tile in range(tiles):
            gsend[0, tile, rws, :] = -total[tile]
            gsend[1, tile, rws, :] = ds[tile]
        return carry

    def place(owner, piece):
        index = owner * pieces + piece
        return index // tiles, lax.rem(index, tiles)

    def band_rows(band, block, offset):
        return pl.ds(pl.multiple_of(offset + (band * per_band + block) * SUB, SUB), SUB)

    def scatter(band):
        def send(step, carry):
            owner = lax.rem(me_s + step, ns)
            for piece in range(pieces):
                block, tile = place(owner, piece)
                pltpu.make_async_remote_copy(
                    src_ref=gsend.at[:, tile, band_rows(band, block, OFF), :],
                    dst_ref=rrx.at[band, ns - 1 - step, piece],
                    send_sem=rs_send.at[band],
                    recv_sem=rs_recv.at[band],
                    device_id={"scen": owner},
                    device_id_type=MESH,
                ).start()
            return carry

        lax.fori_loop(1, ns, send, 0)

    def all_of(band, sem):
        return pltpu.make_async_copy(rrx.at[band], rrx.at[band], sem.at[band])

    def reduce(band):
        if ns > 1:
            all_of(band, rs_recv).wait()
        for piece in range(pieces):
            block, tile = place(me_s, piece)
            src = band_rows(band, block, OFF)
            for kind in range(2):
                terms = [gsend[kind, tile, src, :]]
                terms += [rrx[band, slot, piece, kind] for slot in range(ns - 1)]
                while len(terms) > 1:
                    pairs = [a + b for a, b in zip(terms[0::2], terms[1::2])]
                    terms = pairs + terms[len(pairs) * 2 :]
                factor = planes[PLANE["fac0"] + kind, tile, src, :]
                gfull[kind, tile, band_rows(band, block, 0), :] = terms[0] * factor

        def send(step, carry):
            other = lax.rem(me_s + step, ns)
            for piece in range(pieces):
                block, tile = place(me_s, piece)
                spot = gfull.at[:, tile, band_rows(band, block, 0), :]
                pltpu.make_async_remote_copy(
                    src_ref=spot,
                    dst_ref=spot,
                    send_sem=ag_send.at[band],
                    recv_sem=ag_recv.at[band],
                    device_id={"scen": other},
                    device_id_type=MESH,
                ).start()
            return carry

        lax.fori_loop(1, ns, send, 0)

    def out_copies(band):
        rws = pl.ds(band * per_band * SUB, per_band * SUB)
        return [
            pltpu.make_async_copy(
                outs.at[index, :, rws, :], ref.at[:, rws, :], out_sem.at[band, index]
            )
            for index, ref in enumerate((o_maps, o_first, o_second))
        ]

    def adam(band):
        if ns > 1:
            all_of(band, ag_recv).wait()

        def update(block, carry):
            rws = pl.ds(pl.multiple_of(block * SUB, SUB), SUB)
            src = pl.ds(pl.multiple_of(block * SUB + SUB, SUB), SUB)
            for kind in range(2):
                for tile in range(tiles):
                    cls = pl.ds(tile * LANE, LANE)
                    g = gfull[kind, tile, rws, :]
                    new_first = BETA_FIRST * mom[0, kind, rws, cls] + (1.0 - BETA_FIRST) * g
                    new_second = (
                        BETA_SECOND * mom[1, kind, rws, cls] + (1.0 - BETA_SECOND) * g * g
                    )
                    root = jnp.sqrt(new_second * (1.0 / (1.0 - BETA_SECOND**ADAM_STEP)))
                    scale = LEARN_RATE / (1.0 - BETA_FIRST**ADAM_STEP)
                    outs[0, kind, rws, cls] = raw[MAP0 + kind, src, cls] - (
                        scale * new_first / (root + ADAM_EPS)
                    )
                    outs[1, kind, rws, cls] = new_first
                    outs[2, kind, rws, cls] = new_second
            return carry

        lax.fori_loop(band * per_band, (band + 1) * per_band, update, 0)
        for copy in out_copies(band):
            copy.start()

    for copy in loads[9:]:
        copy.wait()
    last = blocks + 2
    done = [1, 1, 1, 1]
    for band in range(BANDS):
        top_block = 2 + (band + 1) * per_band
        ends = [min(last + 1, top_block + lead) for lead in (3, 2, 1)] + [top_block]
        for index, step in enumerate((pass_one, pass_two, pass_three, pass_four)):
            lax.fori_loop(done[index], ends[index], step, 0)
        done = ends
        scatter(band)
        if band >= 1:
            reduce(band - 1)
        if band >= 2:
            adam(band - 2)
    reduce(BANDS - 1)
    if BANDS >= 2:
        adam(BANDS - 2)
    adam(BANDS - 1)

    for dx in (-1, 1):

        @pl.when(there(dx, 0))
        def _(dx=dx):
            for copy in row_copies(dx):
                copy.wait_send()

    for dx, dy in col_sides:

        @pl.when(there(dx, dy))
        def _(dx=dx, dy=dy):
            col_copy(dx, dy).wait_send()

    for band in range(BANDS):
        if ns > 1:
            all_of(band, rs_send).wait()
            all_of(band, ag_send).wait()
        for copy in out_copies(band):
            copy.wait()


def solution(mesh):
    ns, nx, ny = (mesh.shape[name] for name in ("scen", "lx", "ly"))

    def shards(density, trait, variance, optimum, observed, obs_step, land_code, maps, first, second):
        _, rows, cols = density.shape
        tiles = cols // LANE
        per_band = rows // SUB // BANDS
        pieces = per_band * tiles // ns
        f32 = jnp.float32
        shape = jax.ShapeDtypeStruct(maps.shape, f32)
        hbm = pl.BlockSpec(memory_space=pl.ANY)
        dma = pltpu.SemaphoreType.DMA
        return pl.pallas_call(
            functools.partial(kernel, (ns, nx, ny, rows, cols)),
            out_shape=(shape, shape, shape),
            in_specs=[hbm] * 10,
            out_specs=(hbm, hbm, hbm),
            scratch_shapes=[
                pltpu.VMEM((7, rows + 2 * SUB, cols + LANE), f32),
                pltpu.VMEM((rows + 2 * SUB, cols + LANE), jnp.int32),
                pltpu.VMEM((1, rows), jnp.int32),
                pltpu.VMEM((1, rows), jnp.int32),
                pltpu.VMEM((1, rows), jnp.int32),
                pltpu.VMEM((rows + 2 * SUB, LANE), f32),
                pltpu.VMEM((72, LANE), f32),
                pltpu.VMEM((2, 64, LANE), f32),
                pltpu.VMEM((8, SUB, LANE), f32),
                pltpu.VMEM((LANE, LANE), f32),
                pltpu.VMEM((2, 2, rows, cols), f32),
                pltpu.VMEM((len(NAMES), tiles + 1, rows + 2 * OFF, LANE), f32),
                pltpu.VMEM((2, tiles, rows + 2 * OFF, LANE), f32),
                pltpu.VMEM((BANDS, max(ns - 1, 1), pieces, 2, SUB, LANE), f32),
                pltpu.VMEM((2, tiles, rows, LANE), f32),
                pltpu.VMEM((3, 2, rows, cols), f32),
                dma((11,)),
                dma((2, 8)),
                dma((2, 8)),
                dma((8,)),
                dma((8,)),
                dma((BANDS,)),
                dma((BANDS,)),
                dma((BANDS,)),
                dma((BANDS,)),
                dma((BANDS, 3)),
            ],
            compiler_params=pltpu.CompilerParams(
                collective_id=0, has_side_effects=True, vmem_limit_bytes=56 * 1024 * 1024
            ),
        )(density, trait, variance, optimum, observed, obs_step, land_code, maps, first, second)

    tile = P("scen", "lx", "ly")
    flat = P(None, "lx", "ly")
    return jax.shard_map(
        shards,
        mesh=mesh,
        in_specs=(tile,) * 5 + (P("scen", "lx"), P("lx", "ly"), flat, flat, flat),
        out_specs=(flat, flat, flat),
        check_vma=False,
    )
```

time: 308 us -> 50.3 us (0.16)
  waiting for transfers between devices: 135 us -> 0 us
  blocking collectives: 68.4 us -> 0 us
  starting transfers between devices: 57.4 us -> 0 us
  Pallas kernels: 0 us -> 45.6 us
  other arithmetic: 25 us -> 0 us
  between operations: 14.6 us -> 0.65 us
    reduce_scatter x1 -> x0, waiting for transfers between devices: 75.6 us -> none  [shards(): share = lax.psum_scatter(gradient, 'scen', scatter_dimension=1, tiled=True)]
    all_gather x3 -> x0, blocking collectives: 68.4 us -> none  [the longest x1 23.3 us: shards(): lax.all_gather(maps_part, 'scen', axis=1, tiled=True)]
    ppermute x20 -> x0, waiting for transfers between devices: 59.8 us -> none  [the longest x10 31.4 us: extended(): lax.ppermute(lax.slice_in_dim(block, block.shape[dim] - width, None, axis...]
    ppermute x20 -> x0, starting transfers between devices: 57.3 us -> none  [the longest x10 32.2 us: extended(): lax.ppermute(lax.slice_in_dim(block, block.shape[dim] - width, None, axis...]
    pallas_call x0 -> x1, Pallas kernels: none -> 45.6 us  [shards(): pl.pallas_call(functools.partial(kernel, (ns, nx, ny, rows, cols)), out_s...]
    mul x7 -> x0, other arithmetic: 5.33 us -> none  [the longest x2 4.42 us: advance(): selection = jax.nn.softplus(interior(raw_maps[1]))]
    add_any x2 -> x0, other arithmetic: 4.63 us -> none  [advance(): reach_mid + reach_map[row_cut, col_cut]]
    broadcast_in_dim x5 -> x0, other arithmetic: 4.08 us -> none  [the longest x3 3.18 us: advance(): density_now, trait_now, variance_now = (fields[0], fields[1], fields[2])]
  transfers between devices with their start and end apart: 21 -> 0, of which waited for: 14 -> 0; matrix products, arithmetic and copies ran while one was open for 1% -> 0% of each run, Pallas kernels for 0% -> 0%
where the time goes in v1:
time: 50.3 us; the launch traced here: 50.2 us
  Pallas kernels  45.6 us (91%)
  local copies, waits for them, and re-layouts  3.95 us (8%)
  between operations  0.65 us (1%)
    pallas_call x1, Pallas kernels, shards(): pl.pallas_call(functools.partial(kernel, (ns, nx, ny, rows, cols)), out_s...  45.6 us
    unnamed x7, local copies, waits for them, and re-layouts  3.95 us

profile of v1, /device:TPU:32, one launch (start us, length us, event | category | flops | bytes accessed | tf_op | source)
XLA Modules:
  0.0 50.2 jit_solution(10807240684826480296)
XLA Ops:
  0.6 45.6 %shard_map.121 = (f32[2,128,512]{2,1,0:T(8,128)}, f32[2,128,512]{2,1,0:T(8,128)}, f32[2,128,512]{2,1,0:T(8,128)}) custom-call(f32[1,128,512]{2,1,0:T(8,128)} %dens.1, f32[1,128,512]{2,1,0:T(8,128)} %trait.1, f32[1,128,512]{2,1,0:T(8,128)} %var.1, f32[1,128,512]{2,1,0:T(8,128)} %opt.1, f32[1,128,512]{2,1,0:T(8,128)} %obs.1, s32[1,128]{1,0:T(1,128)} %ostep.1, ...), custom_call_target="tpu_custom_call" | custom-call | tf_op jit(solution)/shard_map/pallas_call | solution.py:699
  46.2 0.0 copy-start.1
  46.2 1.9 %copy.16 = f32[2,128,512]{2,1,0:T(8,128)} copy(f32[2,128,512]{2,1,0:T(8,128)} %get-tuple-element.6) | data formatting | bytes 1048576
  48.1 0.0 copy-done.1
  48.1 0.0 copy-start
  48.1 0.8 %copy.17 = f32[2,128,512]{2,1,0:T(8,128)} copy(f32[2,128,512]{2,1,0:T(8,128)S(1)} %copy-done.1) | data formatting | bytes 1048576
  48.9 0.4 copy-done
  49.4 0.8 %copy.18 = f32[2,128,512]{2,1,0:T(8,128)} copy(f32[2,128,512]{2,1,0:T(8,128)S(1)} %copy-done) | data formatting | bytes 1048576
Async XLA Ops:
  46.2 1.9 %copy-start.1 = (f32[2,128,512]{2,1,0:T(8,128)S(1)}, f32[2,128,512]{2,1,0:T(8,128)}, u32[]{:S(2)}) copy-start(f32[2,128,512]{2,1,0:T(8,128)} %get-tuple-element.7) | copy-start | bytes 1572868
  48.1 1.2 %copy-start = (f32[2,128,512]{2,1,0:T(8,128)S(1)}, f32[2,128,512]{2,1,0:T(8,128)}, u32[]{:S(2)}) copy-start(f32[2,128,512]{2,1,0:T(8,128)} %get-tuple-element.8) | copy-start | bytes 1572868

commit v2 on v1

--- a/solution.py
+++ b/solution.py
@@ -21,12 +21,13 @@
 MESH = pl.DeviceIdType.MESH
 SUB, LANE = 8, 128
 BANDS = 4
+UNROLL = 4
 OFF = 16
 DENS, TRAIT, VAR, OPT, OBS, MAP0, MAP1, LAND = range(8)
 SIDES = [(-1, -1), (-1, 0), (-1, 1), (0, -1), (0, 1), (1, -1), (1, 0), (1, 1)]
 NAMES = (
     "n0", "q0", "m0", "s0", "rho", "lnd", "sel", "wx",
-    "wy", "n1", "q1", "m1", "z1", "s1", "e1", "r1",
+    "ww", "wy", "n1", "q1", "m1", "z1", "s1", "e1", "r1",
     "zs1", "ss1", "u1", "fxn", "fxq", "fxm", "gxn", "gxq",
     "gxm", "ln", "lq", "lm", "kn", "kq", "km", "ds",
     "gx", "gy", "hy", "fac0", "fac1",
@@ -44,11 +45,7 @@
     ostep,
     land,
     maps,
-    first,
-    second,
-    o_maps,
-    o_first,
-    o_second,
+    o_grad,
     raw,
     rawl,
     own_k,
@@ -56,15 +53,13 @@
     down_k,
     krow,
     colsend,
+    cornsend,
     colrx,
     cornrx,
     square,
-    mom,
-    planes,
     gsend,
     rrx,
-    gfull,
-    outs,
+    total,
     load_sem,
     row_send,
     row_recv,
@@ -74,7 +69,8 @@
     rs_recv,
     ag_send,
     ag_recv,
-    out_sem,
+    own_sem,
+    *planes,
 ):
     ns, nx, ny, rows, cols = sizes
     tiles = cols // LANE
@@ -108,8 +104,6 @@
         loads.append((maps.at[slot], raw.at[MAP0 + slot, body, pl.ds(0, cols)]))
     loads.append((land, rawl.at[body, pl.ds(0, cols)]))
     loads.append((ostep, own_k))
-    loads.append((first, mom.at[0]))
-    loads.append((second, mom.at[1]))
     loads = [
         pltpu.make_async_copy(src, dst, load_sem.at[slot])
         for slot, (src, dst) in enumerate(loads)
@@ -134,7 +128,6 @@
 
     over_x = jnp.where(top, 0, 1) + jnp.where(bottom, 0, 1)
     over_y = jnp.where(left, 0, 1) + jnp.where(right, 0, 1)
-    pl.semaphore_wait(barrier, ns - 1 + (over_x + 1) * (over_y + 1) - 1)
 
     def row_copies(dx):
         edge = pl.ds(0, SUB) if dx < 0 else pl.ds(rows - SUB, SUB)
@@ -160,14 +153,7 @@
             for slot, (src, dst) in enumerate(pairs)
         ]
 
-    for dx in (-1, 1):
-
-        @pl.when(there(dx, 0))
-        def _(dx=dx):
-            for copy in row_copies(dx):
-                copy.start()
-
-    for copy in loads[:9]:
+    for copy in loads:
         copy.wait()
 
     def field(slot, rws, cls):
@@ -195,31 +181,12 @@
     for slot in range(8):
         part = turned[8 * slot : 8 * slot + 8, :]
         corner = jnp.where(lane // 8 == slot, pltpu.roll(part, 8 * slot + 4, 1), corner)
-    colsend[0:64, :] = turned[0:64, :]
-    colsend[64:72, :] = corner
-
-    def col_copy(dx, dy):
-        index = SIDES.index((dx, dy))
-        came = SIDES.index((-dx, -dy))
-        if dx == 0:
-            src, dst = colsend.at[0:64, :], colrx.at[0 if dy > 0 else 1]
-        else:
-            src, dst = colsend.at[64:72, :], cornrx.at[came]
-        return pltpu.make_async_remote_copy(
-            src_ref=src,
-            dst_ref=dst,
-            send_sem=col_send.at[index],
-            recv_sem=col_recv.at[came],
-            device_id=target(dx, dy),
-            device_id_type=MESH,
-        )
-
-    col_sides = [side for side in SIDES if side[1]]
-    for dx, dy in col_sides:
-
-        @pl.when(there(dx, dy))
-        def _(dx=dx, dy=dy):
-            col_copy(dx, dy).start()
+    for pair in range(4):
+        even = turned[16 * pair : 16 * pair + 8, :]
+        odd = turned[16 * pair + 8 : 16 * pair + 16, :]
+        colsend[0, 8 * pair : 8 * pair + 8, :] = jnp.where(sub < 4, even, pltpu.roll(odd, 4, 0))
+        colsend[1, 8 * pair : 8 * pair + 8, :] = jnp.where(sub < 4, pltpu.roll(even, 4, 0), odd)
+    cornsend[...] = corner
 
     def prepare(block, lanes):
         src = pl.ds(pl.multiple_of(block * SUB, SUB), SUB)
@@ -230,7 +197,7 @@
             second_moment = v + z * z
 
             def put(name, value):
-                planes[PLANE[name], tile, dst, :] = value
+                planes[PLANE[name]][tile, dst, :] = value
 
             put("n0", n)
             put("q0", n * z)
@@ -251,6 +218,39 @@
         prepare(block, range(tiles))
         return carry
 
+
+    pl.semaphore_wait(barrier, ns - 1 + (over_x + 1) * (over_y + 1) - 1)
+    for dx in (-1, 1):
+
+        @pl.when(there(dx, 0))
+        def _(dx=dx):
+            for copy in row_copies(dx):
+                copy.start()
+
+    def col_copy(dx, dy):
+        index = SIDES.index((dx, dy))
+        came = SIDES.index((-dx, -dy))
+        if dx == 0:
+            way = 0 if dy > 0 else 1
+            src, dst = colsend.at[way], colrx.at[way]
+        else:
+            src, dst = cornsend, cornrx.at[came]
+        return pltpu.make_async_remote_copy(
+            src_ref=src,
+            dst_ref=dst,
+            send_sem=col_send.at[index],
+            recv_sem=col_recv.at[came],
+            device_id=target(dx, dy),
+            device_id_type=MESH,
+        )
+
+    col_sides = [side for side in SIDES if side[1]]
+    for dx, dy in col_sides:
+
+        @pl.when(there(dx, dy))
+        def _(dx=dx, dy=dy):
+            col_copy(dx, dy).start()
+
     lax.fori_loop(1, blocks + 1, prepare_own, 0)
 
     zero = jnp.zeros((SUB, LANE), jnp.float32)
@@ -279,13 +279,19 @@
         @pl.when(jnp.logical_not(there(dx, dy)))
         def _(dx=dx, dy=dy):
             if dx == 0:
-                colrx[0 if dy < 0 else 1] = jnp.zeros((64, LANE), jnp.float32)
+                colrx[0 if dy < 0 else 1] = jnp.zeros((32, LANE), jnp.float32)
             else:
                 cornrx[SIDES.index((dx, dy))] = zero
 
-    for slot in range(8):
-        part = pl.ds(8 * slot, 8)
-        square[part, :] = jnp.where(sub < 4, colrx[0, part, :], colrx[1, part, :])
+    for pair in range(4):
+        part = pl.ds(8 * pair, 8)
+        from_left, from_right = colrx[0, part, :], colrx[1, part, :]
+        square[16 * pair : 16 * pair + 8, :] = jnp.where(
+            sub < 4, from_left, pltpu.roll(from_right, 4, 0)
+        )
+        square[16 * pair + 8 : 16 * pair + 16, :] = jnp.where(
+            sub < 4, pltpu.roll(from_left, 4, 0), from_right
+        )
     upper = lax.rem(lane, 8) < 4
     square[64:72, :] = jnp.where(
         sub < 4,
@@ -357,12 +363,12 @@
                 rws = pl.ds(pl.multiple_of(row, SUB), SUB)
             else:
                 rws = pl.ds(row + shift, SUB)
-            return [planes[PLANE[name], tile, rws, :] for tile in range(wide)]
+            return [planes[PLANE[name]][tile, rws, :] for tile in range(wide)]
 
         def put(name, values):
             rws = pl.ds(pl.multiple_of(row, SUB), SUB)
             for tile, value in enumerate(values):
-                planes[PLANE[name], tile, rws, :] = value
+                planes[PLANE[name]][tile, rws, :] = value
 
         def get_raw(slot):
             rws = pl.ds(pl.multiple_of(row - SUB, SUB), SUB)
@@ -370,20 +376,20 @@
 
         return get, put, get_raw
 
-    def spread(get, name, wx, wy, wyn, keep=None, put=None):
+    def spread(get, name, weights, keep=None, put=None):
+        wx, ww, wy, wyn = weights
         here = get(name)
-        fx = [e - c for e, c in zip(east(here), here)]
+        ahead, behind = east(here), west(here)
+        south, north = get(name, 1), get(name, -1)
+        fx = [e - c for e, c in zip(ahead, here)]
+        fy = [s - c for s, c in zip(south, here)]
         if keep is not None:
             put(keep, fx)
-        flow = [w * f for w, f in zip(wx, fx)]
-        back = west(flow)
-        result = [c + (f - b) for c, f, b in zip(here, flow, back)]
-        south, north = get(name, 1), get(name, -1)
         result = [
-            a + (w * (s - c) + v * (n - c))
-            for a, w, s, c, v, n in zip(result, wy, south, here, wyn, north)
+            c + ((w * f + v * (b - c)) + (y * g + u * (n - c)))
+            for c, w, f, v, b, y, g, u, n in zip(here, wx, fx, ww, behind, wy, fy, wyn, north)
         ]
-        return result, fx, [s - c for s, c in zip(south, here)]
+        return result, fx, fy
 
     def pass_one(block, carry):
         row = block * SUB
@@ -395,17 +401,20 @@
         wy = [(a + b) * (c * d) for a, b, c, d in zip(rho, rho_s, lnd, lnd_s)]
         rho_n, lnd_n = get("rho", -1), get("lnd", -1)
         wyn = [(a + b) * (c * d) for a, b, c, d in zip(rho, rho_n, lnd, lnd_n)]
+        ww = west(wx)
         put("wx", wx)
+        put("ww", ww)
         put("wy", wy)
-        ns_, _, _ = spread(get, "n0", wx, wy, wyn, "fxn", put)
-        qs_, _, _ = spread(get, "q0", wx, wy, wyn, "fxq", put)
-        ms_, _, _ = spread(get, "m0", wx, wy, wyn, "fxm", put)
+        weights = (wx, ww, wy, wyn)
+        ns_, _, _ = spread(get, "n0", weights, "fxn", put)
+        qs_, _, _ = spread(get, "q0", weights, "fxq", put)
+        ms_, _, _ = spread(get, "m0", weights, "fxm", put)
         z, s0, sel, optimum = get_raw(TRAIT), get("s0"), get("sel"), get_raw(OPT)
         rws = pl.ds(pl.multiple_of(row, SUB), SUB)
         for tile in range(wide):
 
             def one(name, value, tile=tile):
-                planes[PLANE[name], tile, rws, :] = value
+                planes[PLANE[name]][tile, rws, :] = value
 
             recip = 1.0 / (ns_[tile] + PRIOR)
             zs = (qs_[tile] + PRIOR * z[tile]) * recip
@@ -436,10 +445,10 @@
     def pass_two(block, carry):
         row = block * SUB
         get, put, get_raw = getter(row)
-        wx, wy, wyn = get("wx"), get("wy"), get("wy", -1)
-        ns_, _, _ = spread(get, "n1", wx, wy, wyn, "gxn", put)
-        qs_, _, _ = spread(get, "q1", wx, wy, wyn, "gxq", put)
-        ms_, _, _ = spread(get, "m1", wx, wy, wyn, "gxm", put)
+        weights = (get("wx"), get("ww"), get("wy"), get("wy", -1))
+        ns_, _, _ = spread(get, "n1", weights, "gxn", put)
+        qs_, _, _ = spread(get, "q1", weights, "gxq", put)
+        ms_, _, _ = spread(get, "m1", weights, "gxm", put)
         z, s1, sel, lnd = get("z1"), get("s1"), get("sel"), get("lnd")
         optimum, observed = get_raw(OPT), get_raw(OBS)
         rws = pl.ds(pl.multiple_of(row, SUB), SUB)
@@ -448,7 +457,7 @@
         for tile in range(wide):
 
             def one(name, value, tile=tile):
-                planes[PLANE[name], tile, rws, :] = value
+                planes[PLANE[name]][tile, rws, :] = value
 
             recip = 1.0 / (ns_[tile] + PRIOR)
             zs = (qs_[tile] + PRIOR * z[tile]) * recip
@@ -472,11 +481,11 @@
     def pass_three(block, carry):
         row = block * SUB
         get, put, get_raw = getter(row)
-        wx, wy, wyn = get("wx"), get("wy"), get("wy", -1)
+        weights = (get("wx"), get("ww"), get("wy"), get("wy", -1))
         spreads = []
         gx = gy = None
         for name, state, kept in (("ln", "n1", "gxn"), ("lq", "q1", "gxq"), ("lm", "m1", "gxm")):
-            result, fx, fy = spread(get, name, wx, wy, wyn)
+            result, fx, fy = spread(get, name, weights)
             spreads.append(result)
             here, south = get(state), get(state, 1)
             px = [a * b for a, b in zip(fx, get(kept))]
@@ -495,7 +504,7 @@
         for tile in range(wide):
 
             def one(name, value, tile=tile):
-                planes[PLANE[name], tile, rws, :] = value
+                planes[PLANE[name]][tile, rws, :] = value
 
             n1, z1, s1, grown, recip, zs, ss, u, sel, lnd, lq, lm, ds = (
                 vals[name][tile] for name in names
@@ -586,17 +595,15 @@
                 while len(terms) > 1:
                     pairs = [a + b for a, b in zip(terms[0::2], terms[1::2])]
                     terms = pairs + terms[len(pairs) * 2 :]
-                factor = planes[PLANE["fac0"] + kind, tile, src, :]
-                gfull[kind, tile, band_rows(band, block, 0), :] = terms[0] * factor
+                factor = planes[PLANE["fac0"] + kind][tile, src, :]
+                total[band, piece, kind] = terms[0] * factor
 
         def send(step, carry):
             other = lax.rem(me_s + step, ns)
             for piece in range(pieces):
-                block, tile = place(me_s, piece)
-                spot = gfull.at[:, tile, band_rows(band, block, 0), :]
                 pltpu.make_async_remote_copy(
-                    src_ref=spot,
-                    dst_ref=spot,
+                    src_ref=total.at[band, piece],
+                    dst_ref=spot(band, piece),
                     send_sem=ag_send.at[band],
                     recv_sem=ag_recv.at[band],
                     device_id={"scen": other},
@@ -605,63 +612,48 @@
             return carry
 
         lax.fori_loop(1, ns, send, 0)
-
-    def out_copies(band):
-        rws = pl.ds(band * per_band * SUB, per_band * SUB)
-        return [
-            pltpu.make_async_copy(
-                outs.at[index, :, rws, :], ref.at[:, rws, :], out_sem.at[band, index]
-            )
-            for index, ref in enumerate((o_maps, o_first, o_second))
-        ]
-
-    def adam(band):
-        if ns > 1:
-            all_of(band, ag_recv).wait()
-
-        def update(block, carry):
-            rws = pl.ds(pl.multiple_of(block * SUB, SUB), SUB)
-            src = pl.ds(pl.multiple_of(block * SUB + SUB, SUB), SUB)
-            for kind in range(2):
-                for tile in range(tiles):
-                    cls = pl.ds(tile * LANE, LANE)
-                    g = gfull[kind, tile, rws, :]
-                    new_first = BETA_FIRST * mom[0, kind, rws, cls] + (1.0 - BETA_FIRST) * g
-                    new_second = (
-                        BETA_SECOND * mom[1, kind, rws, cls] + (1.0 - BETA_SECOND) * g * g
-                    )
-                    root = jnp.sqrt(new_second * (1.0 / (1.0 - BETA_SECOND**ADAM_STEP)))
-                    scale = LEARN_RATE / (1.0 - BETA_FIRST**ADAM_STEP)
-                    outs[0, kind, rws, cls] = raw[MAP0 + kind, src, cls] - (
-                        scale * new_first / (root + ADAM_EPS)
-                    )
-                    outs[1, kind, rws, cls] = new_first
-                    outs[2, kind, rws, cls] = new_second
-            return carry
-
-        lax.fori_loop(band * per_band, (band + 1) * per_band, update, 0)
-        for copy in out_copies(band):
-            copy.start()
-
-    for copy in loads[9:]:
-        copy.wait()
+        for piece in range(pieces):
+            own_copy(band, piece).start()
+
+    def spot(band, piece):
+        block, tile = place(me_s, piece)
+        across = pl.ds(pl.multiple_of(tile * LANE, LANE), LANE)
+        return o_grad.at[:, band_rows(band, block, 0), across]
+
+    def own_copy(band, piece):
+        return pltpu.make_async_copy(
+            total.at[band, piece], spot(band, piece), own_sem.at[band, piece]
+        )
+
+    def run(step, start, stop):
+        whole = (stop - start) // UNROLL
+
+        def several(count):
+            def body(index, carry):
+                for part in range(count):
+                    step(start + index * UNROLL + part, 0)
+                return carry
+
+            return body
+
+        if whole > 0:
+            lax.fori_loop(0, whole, several(UNROLL), 0)
+        rest = (stop - start) - whole * UNROLL
+        if rest > 0:
+            several(rest)(jnp.int32(whole), 0)
+
     last = blocks + 2
     done = [1, 1, 1, 1]
     for band in range(BANDS):
         top_block = 2 + (band + 1) * per_band
         ends = [min(last + 1, top_block + lead) for lead in (3, 2, 1)] + [top_block]
         for index, step in enumerate((pass_one, pass_two, pass_three, pass_four)):
-            lax.fori_loop(done[index], ends[index], step, 0)
+            run(step, done[index], ends[index])
         done = ends
         scatter(band)
         if band >= 1:
             reduce(band - 1)
-        if band >= 2:
-            adam(band - 2)
     reduce(BANDS - 1)
-    if BANDS >= 2:
-        adam(BANDS - 2)
-    adam(BANDS - 1)
 
     for dx in (-1, 1):
 
@@ -680,8 +672,9 @@
         if ns > 1:
             all_of(band, rs_send).wait()
             all_of(band, ag_send).wait()
-        for copy in out_copies(band):
-            copy.wait()
+            all_of(band, ag_recv).wait()
+        for piece in range(pieces):
+            own_copy(band, piece).wait()
 
 
 def solution(mesh):
@@ -694,13 +687,12 @@
         pieces = per_band * tiles // ns
         f32 = jnp.float32
         shape = jax.ShapeDtypeStruct(maps.shape, f32)
-        hbm = pl.BlockSpec(memory_space=pl.ANY)
         dma = pltpu.SemaphoreType.DMA
-        return pl.pallas_call(
+        gradient = pl.pallas_call(
             functools.partial(kernel, (ns, nx, ny, rows, cols)),
-            out_shape=(shape, shape, shape),
-            in_specs=[hbm] * 10,
-            out_specs=(hbm, hbm, hbm),
+            out_shape=shape,
+            in_specs=[pl.BlockSpec(memory_space=pltpu.HBM)] * 8,
+            out_specs=pl.BlockSpec(memory_space=pl.ANY),
             scratch_shapes=[
                 pltpu.VMEM((7, rows + 2 * SUB, cols + LANE), f32),
                 pltpu.VMEM((rows + 2 * SUB, cols + LANE), jnp.int32),
@@ -708,17 +700,15 @@
                 pltpu.VMEM((1, rows), jnp.int32),
                 pltpu.VMEM((1, rows), jnp.int32),
                 pltpu.VMEM((rows + 2 * SUB, LANE), f32),
-                pltpu.VMEM((72, LANE), f32),
-                pltpu.VMEM((2, 64, LANE), f32),
+                pltpu.VMEM((2, 32, LANE), f32),
+                pltpu.VMEM((SUB, LANE), f32),
+                pltpu.VMEM((2, 32, LANE), f32),
                 pltpu.VMEM((8, SUB, LANE), f32),
                 pltpu.VMEM((LANE, LANE), f32),
-                pltpu.VMEM((2, 2, rows, cols), f32),
-                pltpu.VMEM((len(NAMES), tiles + 1, rows + 2 * OFF, LANE), f32),
                 pltpu.VMEM((2, tiles, rows + 2 * OFF, LANE), f32),
                 pltpu.VMEM((BANDS, max(ns - 1, 1), pieces, 2, SUB, LANE), f32),
-                pltpu.VMEM((2, tiles, rows, LANE), f32),
-                pltpu.VMEM((3, 2, rows, cols), f32),
-                dma((11,)),
+                pltpu.VMEM((BANDS, pieces, 2, SUB, LANE), f32),
+                dma((9,)),
                 dma((2, 8)),
                 dma((2, 8)),
                 dma((8,)),
@@ -727,12 +717,19 @@
                 dma((BANDS,)),
                 dma((BANDS,)),
                 dma((BANDS,)),
-                dma((BANDS, 3)),
-            ],
+                dma((BANDS, pieces)),
+            ]
+            + [pltpu.VMEM((tiles + 1, rows + 2 * OFF, LANE), f32)] * len(NAMES),
             compiler_params=pltpu.CompilerParams(
-                collective_id=0, has_side_effects=True, vmem_limit_bytes=56 * 1024 * 1024
+                collective_id=0, has_side_effects=True, vmem_limit_bytes=60 * 1024 * 1024
             ),
-        )(density, trait, variance, optimum, observed, obs_step, land_code, maps, first, second)
+        )(density, trait, variance, optimum, observed, obs_step, land_code, maps)
+        new_first = BETA_FIRST * first + (1.0 - BETA_FIRST) * gradient
+        new_second = BETA_SECOND * second + (1.0 - BETA_SECOND) * gradient * gradient
+        first_hat = new_first / (1.0 - BETA_FIRST**ADAM_STEP)
+        second_hat = new_second / (1.0 - BETA_SECOND**ADAM_STEP)
+        new_maps = maps - LEARN_RATE * first_hat / (jnp.sqrt(second_hat) + ADAM_EPS)
+        return new_maps, new_first, new_second
 
     tile = P("scen", "lx", "ly")
     flat = P(None, "lx", "ly")

time: 50.3 us -> 42.1 us (0.84)
  Pallas kernels: 45.6 us -> 38.9 us
  local copies, waits for them, and re-layouts: 3.95 us -> 0.01 us
  other arithmetic: 0 us -> 2.41 us
    pallas_call x1, Pallas kernels: 45.6 us -> 38.9 us  [shards(): pl.pallas_call(functools.partial(kernel, (ns, nx, ny, rows, cols)), out_s...]
    unnamed x7 -> x6, local copies, waits for them, and re-layouts: 3.95 us -> 0.01 us
    sub x0 -> x1, other arithmetic: none -> 2.41 us  [shards(): new_maps = maps - LEARN_RATE * first_hat / (jnp.sqrt(second_hat) + ADAM_EPS)]
where the time goes in v2:
time: 42.1 us; the launch traced here: 42 us
  Pallas kernels  38.9 us (92%)
  other arithmetic  2.41 us (6%)
  between operations  0.69 us (2%)
    pallas_call x1, Pallas kernels, shards(): pl.pallas_call(functools.partial(kernel, (ns, nx, ny, rows, cols)), out_s...  38.9 us
    sub x1, other arithmetic, shards(): new_maps = maps - LEARN_RATE * first_hat / (jnp.sqrt(second_hat) + ADAM_EPS)  2.41 us

profile of v2, /device:TPU:32, one launch (start us, length us, event | category | flops | bytes accessed | tf_op | source)
XLA Modules:
  0.0 42.0 jit_solution(11858995225322386697)
XLA Ops:
  0.6 0.0 copy-start
  0.6 0.0 copy-start.2
  0.7 0.0 copy-start.1
  0.7 38.9 %shard_map.121 = f32[2,128,512]{2,1,0:T(8,128)} custom-call(f32[1,128,512]{2,1,0:T(8,128)} %dens.1, f32[1,128,512]{2,1,0:T(8,128)} %trait.1, f32[1,128,512]{2,1,0:T(8,128)} %var.1, f32[1,128,512]{2,1,0:T(8,128)} %opt.1, f32[1,128,512]{2,1,0:T(8,128)} %obs.1, s32[1,128]{1,0:T(1,128)} %ostep.1, s32[128,512]{1,0:T(8,128)} %land.1, f32[2,128,512]{2,1,0:T(8,128)} %maps.1), custom_call_target="tpu_custom_call" | custom-call | tf_op jit(solution)/shard_map/pallas_call | solution.py:691
  39.6 0.0 copy-done
  39.6 0.0 copy-done.2
  39.6 0.0 copy-done.1
  39.6 2.4 %divide_subtract_fusion = (f32[2,128,512]{2,1,0:T(8,128)}, f32[2,128,512]{2,1,0:T(8,128)}, f32[2,128,512]{2,1,0:T(8,128)}) fusion(f32[2,128,512]{2,1,0:T(8,128)S(1)} %copy-done, f32[2,128,512]{2,1,0:T(8,128)} %shard_map.121, f32[2,128,512]{2,1,0:T(8,128)S(1)} %copy-done.1, f32[2,128,512]{2,1,0:T(8,128)S(1)} %copy-done.2), kind=kLoop, calls=%fused_computation.2 | loop fusion | flops 1572864 | bytes 3670016 | tf_op jit(solution)/shard_map/sub | solution.py:731
Async XLA Ops:
  0.6 38.9 %copy-start = (f32[2,128,512]{2,1,0:T(8,128)S(1)}, f32[2,128,512]{2,1,0:T(8,128)}, u32[]{:S(2)}) copy-start(f32[2,128,512]{2,1,0:T(8,128)} %maps.1) | copy-start | bytes 1572868
  0.6 38.9 %copy-start.2 = (f32[2,128,512]{2,1,0:T(8,128)S(1)}, f32[2,128,512]{2,1,0:T(8,128)}, u32[]{:S(2)}) copy-start(f32[2,128,512]{2,1,0:T(8,128)} %param.19) | copy-start | bytes 1572868
  0.7 38.9 %copy-start.1 = (f32[2,128,512]{2,1,0:T(8,128)S(1)}, f32[2,128,512]{2,1,0:T(8,128)}, u32[]{:S(2)}) copy-start(f32[2,128,512]{2,1,0:T(8,128)} %param.18) | copy-start | bytes 1572868

commit v3 on v2

--- a/solution.py
+++ b/solution.py
@@ -20,6 +20,7 @@
 
 MESH = pl.DeviceIdType.MESH
 SUB, LANE = 8, 128
+HALO = 4
 BANDS = 4
 UNROLL = 4
 OFF = 16
@@ -130,8 +131,8 @@
     over_y = jnp.where(left, 0, 1) + jnp.where(right, 0, 1)
 
     def row_copies(dx):
-        edge = pl.ds(0, SUB) if dx < 0 else pl.ds(rows - SUB, SUB)
-        halo = pl.ds(rows + SUB, SUB) if dx < 0 else pl.ds(0, SUB)
+        edge = pl.ds(0, HALO) if dx < 0 else pl.ds(rows - HALO, HALO)
+        halo = pl.ds(rows + SUB, HALO) if dx < 0 else pl.ds(SUB - HALO, HALO)
         across = pl.ds(0, cols)
         pairs = [
             (ref.at[0, edge, :], raw.at[slot, halo, across])
@@ -175,7 +176,7 @@
         square[pl.ds(pl.multiple_of(block * SUB, SUB), SUB), :] = packed
         return carry
 
-    lax.fori_loop(0, blocks, pack, 0)
+    lax.fori_loop(0, blocks, pack, 0, unroll=4)
     turned = jnp.transpose(square[...])
     corner = jnp.zeros((SUB, LANE), jnp.float32)
     for slot in range(8):
@@ -251,7 +252,7 @@
         def _(dx=dx, dy=dy):
             col_copy(dx, dy).start()
 
-    lax.fori_loop(1, blocks + 1, prepare_own, 0)
+    lax.fori_loop(1, blocks + 1, prepare_own, 0, unroll=4)
 
     zero = jnp.zeros((SUB, LANE), jnp.float32)
     for dx, halo, kref in ((-1, 0, up_k), (1, rows + SUB, down_k)):
@@ -326,7 +327,7 @@
         krow[rws, :] = jnp.broadcast_to(got[:, 72:73], (SUB, LANE))
         return carry
 
-    lax.fori_loop(0, blocks, unpack, 0)
+    lax.fori_loop(0, blocks, unpack, 0, unroll=4)
     for slot in range(8):
         got = pltpu.roll(square[8 * slot : 8 * slot + 8, :], LANE - 68, 1)
         got = pltpu.roll(got, 4, 0)
@@ -339,7 +340,7 @@
         prepare(block, (tiles,))
         return carry
 
-    lax.fori_loop(0, blocks + 2, prepare_side, 0)
+    lax.fori_loop(0, blocks + 2, prepare_side, 0, unroll=6)
     prepare(0, range(tiles))
     prepare(blocks + 1, range(tiles))
 

time: 42.1 us -> 40.4 us (0.960)
  Pallas kernels: 38.9 us -> 37.1 us
    pallas_call x1, Pallas kernels: 38.9 us -> 37.1 us  [shards(): pl.pallas_call(functools.partial(kernel, (ns, nx, ny, rows, cols)), out_s...]
where the time goes in v3:
time: 40.4 us; the launch traced here: 40.2 us
  Pallas kernels  37.1 us (92%)
  other arithmetic  2.41 us (6%)
  between operations  0.69 us (2%)
    pallas_call x1, Pallas kernels, shards(): pl.pallas_call(functools.partial(kernel, (ns, nx, ny, rows, cols)), out_s...  37.1 us
    sub x1, other arithmetic, shards(): new_maps = maps - LEARN_RATE * first_hat / (jnp.sqrt(second_hat) + ADAM_EPS)  2.41 us

profile of v3, /device:TPU:32, one launch (start us, length us, event | category | flops | bytes accessed | tf_op | source)
XLA Modules:
  0.0 40.2 jit_solution(2654924939529687919)
XLA Ops:
  0.6 0.0 copy-start
  0.6 0.0 copy-start.2
  0.7 0.0 copy-start.1
  0.7 37.1 %shard_map.121 = f32[2,128,512]{2,1,0:T(8,128)} custom-call(f32[1,128,512]{2,1,0:T(8,128)} %dens.1, f32[1,128,512]{2,1,0:T(8,128)} %trait.1, f32[1,128,512]{2,1,0:T(8,128)} %var.1, f32[1,128,512]{2,1,0:T(8,128)} %opt.1, f32[1,128,512]{2,1,0:T(8,128)} %obs.1, s32[1,128]{1,0:T(1,128)} %ostep.1, s32[128,512]{1,0:T(8,128)} %land.1, f32[2,128,512]{2,1,0:T(8,128)} %maps.1), custom_call_target="tpu_custom_call" | custom-call | tf_op jit(solution)/shard_map/pallas_call | solution.py:692
  37.8 0.0 copy-done
  37.8 0.0 copy-done.2
  37.8 0.0 copy-done.1
  37.8 2.4 %divide_subtract_fusion = (f32[2,128,512]{2,1,0:T(8,128)}, f32[2,128,512]{2,1,0:T(8,128)}, f32[2,128,512]{2,1,0:T(8,128)}) fusion(f32[2,128,512]{2,1,0:T(8,128)S(1)} %copy-done, f32[2,128,512]{2,1,0:T(8,128)} %shard_map.121, f32[2,128,512]{2,1,0:T(8,128)S(1)} %copy-done.1, f32[2,128,512]{2,1,0:T(8,128)S(1)} %copy-done.2), kind=kLoop, calls=%fused_computation.2 | loop fusion | flops 1572864 | bytes 3670016 | tf_op jit(solution)/shard_map/sub | solution.py:732
Async XLA Ops:
  0.6 37.1 %copy-start = (f32[2,128,512]{2,1,0:T(8,128)S(1)}, f32[2,128,512]{2,1,0:T(8,128)}, u32[]{:S(2)}) copy-start(f32[2,128,512]{2,1,0:T(8,128)} %maps.1) | copy-start | bytes 1572868
  0.6 37.1 %copy-start.2 = (f32[2,128,512]{2,1,0:T(8,128)S(1)}, f32[2,128,512]{2,1,0:T(8,128)}, u32[]{:S(2)}) copy-start(f32[2,128,512]{2,1,0:T(8,128)} %param.19) | copy-start | bytes 1572868
  0.7 37.1 %copy-start.1 = (f32[2,128,512]{2,1,0:T(8,128)S(1)}, f32[2,128,512]{2,1,0:T(8,128)}, u32[]{:S(2)}) copy-start(f32[2,128,512]{2,1,0:T(8,128)} %param.18) | copy-start | bytes 1572868

commit v4 on v3

--- a/solution.py
+++ b/solution.py
@@ -221,13 +221,6 @@
 
 
     pl.semaphore_wait(barrier, ns - 1 + (over_x + 1) * (over_y + 1) - 1)
-    for dx in (-1, 1):
-
-        @pl.when(there(dx, 0))
-        def _(dx=dx):
-            for copy in row_copies(dx):
-                copy.start()
-
     def col_copy(dx, dy):
         index = SIDES.index((dx, dy))
         came = SIDES.index((-dx, -dy))
@@ -252,8 +245,16 @@
         def _(dx=dx, dy=dy):
             col_copy(dx, dy).start()
 
+    for dx in (-1, 1):
+
+        @pl.when(there(dx, 0))
+        def _(dx=dx):
+            for copy in row_copies(dx):
+                copy.start()
+
     lax.fori_loop(1, blocks + 1, prepare_own, 0, unroll=4)
 
+    soon = min(blocks, 2 * per_band)
     zero = jnp.zeros((SUB, LANE), jnp.float32)
     for dx, halo, kref in ((-1, 0, up_k), (1, rows + SUB, down_k)):
 
@@ -327,7 +328,7 @@
         krow[rws, :] = jnp.broadcast_to(got[:, 72:73], (SUB, LANE))
         return carry
 
-    lax.fori_loop(0, blocks, unpack, 0, unroll=4)
+    lax.fori_loop(0, soon, unpack, 0, unroll=4)
     for slot in range(8):
         got = pltpu.roll(square[8 * slot : 8 * slot + 8, :], LANE - 68, 1)
         got = pltpu.roll(got, 4, 0)
@@ -340,9 +341,14 @@
         prepare(block, (tiles,))
         return carry
 
-    lax.fori_loop(0, blocks + 2, prepare_side, 0, unroll=6)
+    lax.fori_loop(0, soon + 1, prepare_side, 0, unroll=3)
     prepare(0, range(tiles))
-    prepare(blocks + 1, range(tiles))
+
+    def finish_halo():
+        lax.fori_loop(soon, blocks, unpack, 0, unroll=4)
+        lax.fori_loop(soon + 1, blocks + 2, prepare_side, 0, unroll=3)
+        prepare(blocks + 1, range(tiles))
+
 
     def east(values):
         turned = [pltpu.roll(value, LANE - 1, 1) for value in values]
@@ -652,6 +658,8 @@
             run(step, done[index], ends[index])
         done = ends
         scatter(band)
+        if band == 0:
+            finish_halo()
         if band >= 1:
             reduce(band - 1)
     reduce(BANDS - 1)

time: 40.4 us -> 39.5 us (0.978)
  the two profiles are of different devices: /device:TPU:32 before, /device:TPU:8 now
where the time goes in v4:
time: 39.5 us; the launch traced here: 39.3 us
  Pallas kernels  36.2 us (92%)
  other arithmetic  2.41 us (6%)
  between operations  0.69 us (2%)
    pallas_call x1, Pallas kernels, shards(): pl.pallas_call(functools.partial(kernel, (ns, nx, ny, rows, cols)), out_s...  36.2 us
    sub x1, other arithmetic, shards(): new_maps = maps - LEARN_RATE * first_hat / (jnp.sqrt(second_hat) + ADAM_EPS)  2.41 us

profile of v4, /device:TPU:8, one launch (start us, length us, event | category | flops | bytes accessed | tf_op | source)
XLA Modules:
  0.0 39.3 jit_solution(4288049613373053283)
XLA Ops:
  0.6 0.0 copy-start
  0.6 0.0 copy-start.2
  0.7 0.0 copy-start.1
  0.7 36.2 %shard_map.121 = f32[2,128,512]{2,1,0:T(8,128)} custom-call(f32[1,128,512]{2,1,0:T(8,128)} %dens.1, f32[1,128,512]{2,1,0:T(8,128)} %trait.1, f32[1,128,512]{2,1,0:T(8,128)} %var.1, f32[1,128,512]{2,1,0:T(8,128)} %opt.1, f32[1,128,512]{2,1,0:T(8,128)} %obs.1, s32[1,128]{1,0:T(1,128)} %ostep.1, s32[128,512]{1,0:T(8,128)} %land.1, f32[2,128,512]{2,1,0:T(8,128)} %maps.1), custom_call_target="tpu_custom_call" | custom-call | tf_op jit(solution)/shard_map/pallas_call | solution.py:700
  36.9 0.0 copy-done
  36.9 0.0 copy-done.2
  36.9 0.0 copy-done.1
  36.9 2.4 %divide_subtract_fusion = (f32[2,128,512]{2,1,0:T(8,128)}, f32[2,128,512]{2,1,0:T(8,128)}, f32[2,128,512]{2,1,0:T(8,128)}) fusion(f32[2,128,512]{2,1,0:T(8,128)S(1)} %copy-done, f32[2,128,512]{2,1,0:T(8,128)} %shard_map.121, f32[2,128,512]{2,1,0:T(8,128)S(1)} %copy-done.1, f32[2,128,512]{2,1,0:T(8,128)S(1)} %copy-done.2), kind=kLoop, calls=%fused_computation.2 | loop fusion | flops 1572864 | bytes 3670016 | tf_op jit(solution)/shard_map/sub | solution.py:740
Async XLA Ops:
  0.6 36.3 %copy-start = (f32[2,128,512]{2,1,0:T(8,128)S(1)}, f32[2,128,512]{2,1,0:T(8,128)}, u32[]{:S(2)}) copy-start(f32[2,128,512]{2,1,0:T(8,128)} %maps.1) | copy-start | bytes 1572868
  0.6 36.3 %copy-start.2 = (f32[2,128,512]{2,1,0:T(8,128)S(1)}, f32[2,128,512]{2,1,0:T(8,128)}, u32[]{:S(2)}) copy-start(f32[2,128,512]{2,1,0:T(8,128)} %param.19) | copy-start | bytes 1572868
  0.7 36.3 %copy-start.1 = (f32[2,128,512]{2,1,0:T(8,128)S(1)}, f32[2,128,512]{2,1,0:T(8,128)}, u32[]{:S(2)}) copy-start(f32[2,128,512]{2,1,0:T(8,128)} %param.18) | copy-start | bytes 1572868

commit v5 on v4

--- a/solution.py
+++ b/solution.py
@@ -660,9 +660,8 @@
         scatter(band)
         if band == 0:
             finish_halo()
-        if band >= 1:
-            reduce(band - 1)
-    reduce(BANDS - 1)
+    for band in range(BANDS):
+        reduce(band)
 
     for dx in (-1, 1):
 

time: 39.5 us -> 36.5 us (0.924)
  the two profiles are of different devices: /device:TPU:8 before, /device:TPU:1 now
where the time goes in v5:
time: 36.5 us; the launch traced here: 36.4 us
  Pallas kernels  33.3 us (91%)
  other arithmetic  2.41 us (7%)
  between operations  0.69 us (2%)
    pallas_call x1, Pallas kernels, shards(): pl.pallas_call(functools.partial(kernel, (ns, nx, ny, rows, cols)), out_s...  33.3 us
    sub x1, other arithmetic, shards(): new_maps = maps - LEARN_RATE * first_hat / (jnp.sqrt(second_hat) + ADAM_EPS)  2.41 us

profile of v5, /device:TPU:1, one launch (start us, length us, event | category | flops | bytes accessed | tf_op | source)
XLA Modules:
  0.0 36.4 jit_solution(7869004452665645633)
XLA Ops:
  0.6 0.0 copy-start
  0.6 0.0 copy-start.2
  0.7 0.0 copy-start.1
  0.7 33.3 %shard_map.121 = f32[2,128,512]{2,1,0:T(8,128)} custom-call(f32[1,128,512]{2,1,0:T(8,128)} %dens.1, f32[1,128,512]{2,1,0:T(8,128)} %trait.1, f32[1,128,512]{2,1,0:T(8,128)} %var.1, f32[1,128,512]{2,1,0:T(8,128)} %opt.1, f32[1,128,512]{2,1,0:T(8,128)} %obs.1, s32[1,128]{1,0:T(1,128)} %ostep.1, s32[128,512]{1,0:T(8,128)} %land.1, f32[2,128,512]{2,1,0:T(8,128)} %maps.1), custom_call_target="tpu_custom_call" | custom-call | tf_op jit(solution)/shard_map/pallas_call | solution.py:699
  33.9 0.0 copy-done
  34.0 0.0 copy-done.2
  34.0 0.0 copy-done.1
  34.0 2.4 %divide_subtract_fusion = (f32[2,128,512]{2,1,0:T(8,128)}, f32[2,128,512]{2,1,0:T(8,128)}, f32[2,128,512]{2,1,0:T(8,128)}) fusion(f32[2,128,512]{2,1,0:T(8,128)S(1)} %copy-done, f32[2,128,512]{2,1,0:T(8,128)} %shard_map.121, f32[2,128,512]{2,1,0:T(8,128)S(1)} %copy-done.1, f32[2,128,512]{2,1,0:T(8,128)S(1)} %copy-done.2), kind=kLoop, calls=%fused_computation.2 | loop fusion | flops 1572864 | bytes 3670016 | tf_op jit(solution)/shard_map/sub | solution.py:739
Async XLA Ops:
  0.6 33.3 %copy-start = (f32[2,128,512]{2,1,0:T(8,128)S(1)}, f32[2,128,512]{2,1,0:T(8,128)}, u32[]{:S(2)}) copy-start(f32[2,128,512]{2,1,0:T(8,128)} %maps.1) | copy-start | bytes 1572868
  0.6 33.3 %copy-start.2 = (f32[2,128,512]{2,1,0:T(8,128)S(1)}, f32[2,128,512]{2,1,0:T(8,128)}, u32[]{:S(2)}) copy-start(f32[2,128,512]{2,1,0:T(8,128)} %param.19) | copy-start | bytes 1572868
  0.7 33.3 %copy-start.1 = (f32[2,128,512]{2,1,0:T(8,128)S(1)}, f32[2,128,512]{2,1,0:T(8,128)}, u32[]{:S(2)}) copy-start(f32[2,128,512]{2,1,0:T(8,128)} %param.18) | copy-start | bytes 1572868
